TPU v7x, 256 devices: a whole 4x4x8 slice. The times are simulated.
256 devices in a mesh: slab: 16 (over z_hi, x, core), space: 16 (over z_lo, y).
Axes of the slice: x: 4, y: 4, z: 8 (z_hi: 2, z_lo: 4; z = z_hi * 4 + z_lo), core: 2. Of those that a mesh axis runs over, the one named last changes fastest.
Arguments:
- state_old: float32 [16, 3, 32, 128, 128], P('slab', None, 'space'), may hold values from -6 to 6
- coarse_old: float32 [16, 3, 32, 128, 128], P('slab', None, 'space'), may hold values from -6 to 6
- source: float32 [16, 3, 32, 128, 128], P('slab', None, 'space'), may hold values from -3 to 3
- start_state: float32 [3, 32, 128, 128], P(None, 'space'), may hold values from -6 to 6
- conduct: float32 [32, 128, 128], P('space'), may hold values from 0.05 to 1
- reluct: float32 [32, 128, 128], P('space'), may hold values from 0.25 to 1
- converged: int32 [1], replicated, may hold values from 0 to 16383
Outputs:
- state_new: float32 [16, 3, 32, 128, 128], P('slab', None, 'space')
- coarse_new: float32 [16, 3, 32, 128, 128], P('slab', None, 'space')
Inputs may be any that keep to these rules, and one draw needn't show every extreme that they name: converged mod 16 names the slab group that has converged.
All inputs are finite; a program needn't handle non-finite values.
Results may differ from a plain program's by a relative error of at most 0.0003.
Values sent between devices are 32-bit elements; how exact they have to be, the bound alone decides.
No kernel may reach another device: no remote copies, remote signals or barrier semaphores. Data moves between devices by JAX's collectives and lax.ppermute only.
A program may use at most 64 MiB of HBM per device.

v0:
```python
import jax
import jax.numpy as jnp
from jax import lax
from jax.sharding import PartitionSpec as P

FSTEPS = 2
FSWEEPS = 8
CSWEEPS = 2


floor_rate = 0.05
top_rate = 1.0
curl_bound = 14.0


def from_behind(value, axis, steps):
    count = lax.axis_size(axis)
    first, last = (max(0, -steps), min(count, count - steps))
    return lax.ppermute(value, axis, [(source, source + steps) for source in range(first, last)])


def from_behind_2(block, axis, distance):
    devices = range(lax.axis_size(axis))
    route = [((i - distance) % len(devices), i) for i in devices]
    return lax.ppermute(block, axis, route)


def forward(array, along, border):
    interior = lax.slice_in_dim(array, 1, array.shape[along], axis=along)
    return jnp.concatenate((interior, border), along) - array


def backward(array, along, border):
    interior = lax.slice_in_dim(array, 0, array.shape[along] - 1, axis=along)
    return jnp.concatenate((border, interior), along) - array


def zero_plane(array, along):
    return jnp.zeros_like(lax.slice_in_dim(array, 0, 1, axis=along))


def chebyshev(target, initial, mass_term, lower_bound, upper_bound, sweeps, operator):
    center = 0.5 * (upper_bound + lower_bound)
    radius = 0.5 * (upper_bound - lower_bound)
    spread = center / radius
    rho_now = 1.0 / spread
    residual = target - operator(initial, mass_term)
    iterate = initial
    update = residual / center
    for repeat in range(sweeps):
        iterate = iterate + update
        if repeat + 1 < sweeps:
            residual = residual - operator(update, mass_term)
            rho_next = 1.0 / (2.0 * spread - rho_now)
            update = rho_next * rho_now * update + 2.0 * rho_next / radius * residual
            rho_now = rho_next
    return iterate


def local(state_old, coarse_old, source, start_state, conduct, reluct, converged):
    groups = lax.axis_size("slab")
    own_index = lax.axis_index("slab")
    done_group = converged[0] % groups
    position = (own_index - done_group - 1) % groups

    def operate(edge_field, mass_term):
        x_part, y_part, z_part = (edge_field[0], edge_field[1], edge_field[2])
        above_planes = from_behind(edge_field[1:3, 0:1], "space", -1)
        y_above = above_planes[0]
        z_above = above_planes[1]
        curl_x = reluct * (
            forward(z_part, 1, zero_plane(z_part, 1)) - forward(y_part, 2, zero_plane(y_part, 2))
        )
        curl_y = reluct * (forward(x_part, 2, zero_plane(x_part, 2)) - forward(z_part, 0, z_above))
        curl_z = reluct * (forward(y_part, 0, y_above) - forward(x_part, 1, zero_plane(x_part, 1)))
        from_below = from_behind(jnp.stack((curl_y[-1:], curl_z[-1:])), "space", 1)
        low_y = from_below[0]
        low_z = from_below[1]
        k_x = backward(curl_y, 2, zero_plane(curl_y, 2)) - backward(
            curl_z, 1, zero_plane(curl_z, 1)
        )
        k_y = backward(curl_z, 0, low_z) - backward(curl_x, 2, zero_plane(curl_x, 2))
        k_z = backward(curl_x, 1, zero_plane(curl_x, 1)) - backward(curl_y, 0, low_y)
        return mass_term * edge_field + jnp.stack((k_x, k_y, k_z))

    fine_mass = FSTEPS * conduct
    fine_floor = FSTEPS * floor_rate
    fine_top = FSTEPS * top_rate + curl_bound
    coarse_top = top_rate + curl_bound
    slab_source = source[0]
    iterate = state_old[0]
    for repeat in range(FSTEPS):
        iterate = chebyshev(
            fine_mass * iterate + slab_source,
            iterate,
            fine_mass,
            fine_floor,
            fine_top,
            FSWEEPS,
            operate,
        )
    correction = iterate - coarse_old[0]

    def coarse_full(begin_state):
        return chebyshev(
            conduct * begin_state + slab_source,
            begin_state,
            conduct,
            floor_rate,
            coarse_top,
            CSWEEPS,
            operate,
        )

    def link_turn(counter, incoming):
        outgoing = coarse_full(incoming) + correction
        received = from_behind_2(outgoing, "slab", 1)
        return jnp.where(position == 0, start_state, received)

    chained = lax.fori_loop(0, groups - 1, link_turn, start_state)
    coarse_new = coarse_full(chained)
    return (chained[None], coarse_new[None])


def solution(mesh):
    placed = (
        P("slab", None, "space", None, None),
        P("slab", None, "space", None, None),
        P("slab", None, "space", None, None),
        P(None, "space", None, None),
        P("space", None, None),
        P("space", None, None),
        P(),
    )
    return jax.shard_map(
        local,
        mesh=mesh,
        in_specs=placed,
        out_specs=(P("slab", None, "space", None, None), P("slab", None, "space", None, None)),
        check_vma=False,
    )
```

profile of v0, /device:TPU:160, one launch (start us, length us, event | category | flops | bytes accessed | tf_op | source)
XLA Modules:
  0.0 1079.1 jit_solution(10677288169642173136)
XLA Ops:
  114.5 7.7 collective-permute-done.18
  233.8 8.0 collective-permute-done.32
  251.6 8.5 collective-permute-done.34
  281.9 758.5 %while.12 = (s32[]{:T(128)}, f32[3,2,128,128]{3,2,1,0:T(8,128)S(1)}, pred[]{:T(512)}, f32[2,128,128]{2,1,0:T(8,128)S(1)}, f32[3,2,128,128]{3,2,1,0:T(8,128)S(1)}...) while((s32[]{:T(128)}, ...), condition=%wide.region_1.2_spmd, body=%wide.region_0.1_spmd.sunk | while | flops 4292610 | bytes 23298340 | solution.py:120
  315.0 18.9 %collective-permute-done.4 = f32[3,2,128,128]{3,2,1,0:T(8,128)S(1)} collective-permute-done((f32[3,2,128,128]{3,2,1,0:T(8,128)S(1)}, f32[3,2,128,128]{3,2,1,0:T(8,128)S(1)}, u32[]{:S(2)}, u32[]{:S(2)}) %collective-permute-start.4) | collective-permute-done | bytes 393248 | tf_op jit(solution)/shard_map/while/body/eval_jaxpr/ppermute | solution.py:25
  343.1 8.4 collective-permute-done.1
  368.5 15.1 %collective-permute-done.4 = f32[3,2,128,128]{3,2,1,0:T(8,128)S(1)} collective-permute-done((f32[3,2,128,128]{3,2,1,0:T(8,128)S(1)}, f32[3,2,128,128]{3,2,1,0:T(8,128)S(1)}, u32[]{:S(2)}, u32[]{:S(2)}) %collective-permute-start.4) | collective-permute-done | bytes 393248 | tf_op jit(solution)/shard_map/while/body/eval_jaxpr/ppermute | solution.py:25
  418.4 13.5 %collective-permute-done.4 = f32[3,2,128,128]{3,2,1,0:T(8,128)S(1)} collective-permute-done((f32[3,2,128,128]{3,2,1,0:T(8,128)S(1)}, f32[3,2,128,128]{3,2,1,0:T(8,128)S(1)}, u32[]{:S(2)}, u32[]{:S(2)}) %collective-permute-start.4) | collective-permute-done | bytes 393248 | tf_op jit(solution)/shard_map/while/body/eval_jaxpr/ppermute | solution.py:25
  468.1 13.3 %collective-permute-done.4 = f32[3,2,128,128]{3,2,1,0:T(8,128)S(1)} collective-permute-done((f32[3,2,128,128]{3,2,1,0:T(8,128)S(1)}, f32[3,2,128,128]{3,2,1,0:T(8,128)S(1)}, u32[]{:S(2)}, u32[]{:S(2)}) %collective-permute-start.4) | collective-permute-done | bytes 393248 | tf_op jit(solution)/shard_map/while/body/eval_jaxpr/ppermute | solution.py:25
  493.3 8.3 collective-permute-done.1
  518.6 13.2 %collective-permute-done.4 = f32[3,2,128,128]{3,2,1,0:T(8,128)S(1)} collective-permute-done((f32[3,2,128,128]{3,2,1,0:T(8,128)S(1)}, f32[3,2,128,128]{3,2,1,0:T(8,128)S(1)}, u32[]{:S(2)}, u32[]{:S(2)}) %collective-permute-start.4) | collective-permute-done | bytes 393248 | tf_op jit(solution)/shard_map/while/body/eval_jaxpr/ppermute | solution.py:25
  531.9 7.7 collective-permute-start
  568.7 13.3 %collective-permute-done.4 = f32[3,2,128,128]{3,2,1,0:T(8,128)S(1)} collective-permute-done((f32[3,2,128,128]{3,2,1,0:T(8,128)S(1)}, f32[3,2,128,128]{3,2,1,0:T(8,128)S(1)}, u32[]{:S(2)}, u32[]{:S(2)}) %collective-permute-start.4) | collective-permute-done | bytes 393248 | tf_op jit(solution)/shard_map/while/body/eval_jaxpr/ppermute | solution.py:25
  582.1 9.3 collective-permute-start
  620.5 13.3 %collective-permute-done.4 = f32[3,2,128,128]{3,2,1,0:T(8,128)S(1)} collective-permute-done((f32[3,2,128,128]{3,2,1,0:T(8,128)S(1)}, f32[3,2,128,128]{3,2,1,0:T(8,128)S(1)}, u32[]{:S(2)}, u32[]{:S(2)}) %collective-permute-start.4) | collective-permute-done | bytes 393248 | tf_op jit(solution)/shard_map/while/body/eval_jaxpr/ppermute | solution.py:25
  633.9 9.4 collective-permute-start
  672.4 13.3 %collective-permute-done.4 = f32[3,2,128,128]{3,2,1,0:T(8,128)S(1)} collective-permute-done((f32[3,2,128,128]{3,2,1,0:T(8,128)S(1)}, f32[3,2,128,128]{3,2,1,0:T(8,128)S(1)}, u32[]{:S(2)}, u32[]{:S(2)}) %collective-permute-start.4) | collective-permute-done | bytes 393248 | tf_op jit(solution)/shard_map/while/body/eval_jaxpr/ppermute | solution.py:25
  685.8 8.6 collective-permute-start
  723.5 13.3 %collective-permute-done.4 = f32[3,2,128,128]{3,2,1,0:T(8,128)S(1)} collective-permute-done((f32[3,2,128,128]{3,2,1,0:T(8,128)S(1)}, f32[3,2,128,128]{3,2,1,0:T(8,128)S(1)}, u32[]{:S(2)}, u32[]{:S(2)}) %collective-permute-start.4) | collective-permute-done | bytes 393248 | tf_op jit(solution)/shard_map/while/body/eval_jaxpr/ppermute | solution.py:25
  736.9 8.2 collective-permute-start
  774.2 13.3 %collective-permute-done.4 = f32[3,2,128,128]{3,2,1,0:T(8,128)S(1)} collective-permute-done((f32[3,2,128,128]{3,2,1,0:T(8,128)S(1)}, f32[3,2,128,128]{3,2,1,0:T(8,128)S(1)}, u32[]{:S(2)}, u32[]{:S(2)}) %collective-permute-start.4) | collective-permute-done | bytes 393248 | tf_op jit(solution)/shard_map/while/body/eval_jaxpr/ppermute | solution.py:25
  787.6 7.9 collective-permute-start
  824.6 13.3 %collective-permute-done.4 = f32[3,2,128,128]{3,2,1,0:T(8,128)S(1)} collective-permute-done((f32[3,2,128,128]{3,2,1,0:T(8,128)S(1)}, f32[3,2,128,128]{3,2,1,0:T(8,128)S(1)}, u32[]{:S(2)}, u32[]{:S(2)}) %collective-permute-start.4) | collective-permute-done | bytes 393248 | tf_op jit(solution)/shard_map/while/body/eval_jaxpr/ppermute | solution.py:25
  838.0 8.2 collective-permute-start
  875.2 13.3 %collective-permute-done.4 = f32[3,2,128,128]{3,2,1,0:T(8,128)S(1)} collective-permute-done((f32[3,2,128,128]{3,2,1,0:T(8,128)S(1)}, f32[3,2,128,128]{3,2,1,0:T(8,128)S(1)}, u32[]{:S(2)}, u32[]{:S(2)}) %collective-permute-start.4) | collective-permute-done | bytes 393248 | tf_op jit(solution)/shard_map/while/body/eval_jaxpr/ppermute | solution.py:25
  888.6 8.2 collective-permute-start
  925.9 13.3 %collective-permute-done.4 = f32[3,2,128,128]{3,2,1,0:T(8,128)S(1)} collective-permute-done((f32[3,2,128,128]{3,2,1,0:T(8,128)S(1)}, f32[3,2,128,128]{3,2,1,0:T(8,128)S(1)}, u32[]{:S(2)}, u32[]{:S(2)}) %collective-permute-start.4) | collective-permute-done | bytes 393248 | tf_op jit(solution)/shard_map/while/body/eval_jaxpr/ppermute | solution.py:25
  939.3 8.2 collective-permute-start
  976.5 13.3 %collective-permute-done.4 = f32[3,2,128,128]{3,2,1,0:T(8,128)S(1)} collective-permute-done((f32[3,2,128,128]{3,2,1,0:T(8,128)S(1)}, f32[3,2,128,128]{3,2,1,0:T(8,128)S(1)}, u32[]{:S(2)}, u32[]{:S(2)}) %collective-permute-start.4) | collective-permute-done | bytes 393248 | tf_op jit(solution)/shard_map/while/body/eval_jaxpr/ppermute | solution.py:25
  989.9 8.1 collective-permute-start
  1027.1 13.3 %collective-permute-done.4 = f32[3,2,128,128]{3,2,1,0:T(8,128)S(1)} collective-permute-done((f32[3,2,128,128]{3,2,1,0:T(8,128)S(1)}, f32[3,2,128,128]{3,2,1,0:T(8,128)S(1)}, u32[]{:S(2)}, u32[]{:S(2)}) %collective-permute-start.4) | collective-permute-done | bytes 393248 | tf_op jit(solution)/shard_map/while/body/eval_jaxpr/ppermute | solution.py:25
  1040.7 7.9 collective-permute-start.37
  (987 shorter events, 731.3 us)
Async XLA Ops:
  112.6 9.6 collective-permute-start.18
  231.7 10.1 collective-permute-start.32
  249.7 10.4 collective-permute-start.34
  314.9 19.0 %collective-permute-start.4 = (f32[3,2,128,128]{3,2,1,0:T(8,128)S(1)}, f32[3,2,128,128]{3,2,1,0:T(8,128)S(1)}, u32[]{:S(2)}, u32[]{:S(2)}) collective-permute-start(f32[3,2,128,128]{3,2,1,0:T(8,128)S(1)} %fusion.224), channel_id=1, source_target_pairs={{240,0},{0,16},{16,32},{32,48},{48,64},{64,80},{80,96},{96,112},{1... | collective-permute-start | bytes 1179656 | tf_op jit(solution)/shard_map/while/body/eval_jaxpr/ppermute | solution.py:25
  341.1 10.3 collective-permute-start.1
  368.4 15.2 %collective-permute-start.4 = (f32[3,2,128,128]{3,2,1,0:T(8,128)S(1)}, f32[3,2,128,128]{3,2,1,0:T(8,128)S(1)}, u32[]{:S(2)}, u32[]{:S(2)}) collective-permute-start(f32[3,2,128,128]{3,2,1,0:T(8,128)S(1)} %fusion.224), channel_id=1, source_target_pairs={{240,0},{0,16},{16,32},{32,48},{48,64},{64,80},{80,96},{96,112},{1... | collective-permute-start | bytes 1179656 | tf_op jit(solution)/shard_map/while/body/eval_jaxpr/ppermute | solution.py:25
  418.3 13.6 %collective-permute-start.4 = (f32[3,2,128,128]{3,2,1,0:T(8,128)S(1)}, f32[3,2,128,128]{3,2,1,0:T(8,128)S(1)}, u32[]{:S(2)}, u32[]{:S(2)}) collective-permute-start(f32[3,2,128,128]{3,2,1,0:T(8,128)S(1)} %fusion.224), channel_id=1, source_target_pairs={{240,0},{0,16},{16,32},{32,48},{48,64},{64,80},{80,96},{96,112},{1... | collective-permute-start | bytes 1179656 | tf_op jit(solution)/shard_map/while/body/eval_jaxpr/ppermute | solution.py:25
  468.0 13.4 %collective-permute-start.4 = (f32[3,2,128,128]{3,2,1,0:T(8,128)S(1)}, f32[3,2,128,128]{3,2,1,0:T(8,128)S(1)}, u32[]{:S(2)}, u32[]{:S(2)}) collective-permute-start(f32[3,2,128,128]{3,2,1,0:T(8,128)S(1)} %fusion.224), channel_id=1, source_target_pairs={{240,0},{0,16},{16,32},{32,48},{48,64},{64,80},{80,96},{96,112},{1... | collective-permute-start | bytes 1179656 | tf_op jit(solution)/shard_map/while/body/eval_jaxpr/ppermute | solution.py:25
  481.5 9.8 collective-permute-start
  491.4 10.2 collective-permute-start.1
  518.5 13.3 %collective-permute-start.4 = (f32[3,2,128,128]{3,2,1,0:T(8,128)S(1)}, f32[3,2,128,128]{3,2,1,0:T(8,128)S(1)}, u32[]{:S(2)}, u32[]{:S(2)}) collective-permute-start(f32[3,2,128,128]{3,2,1,0:T(8,128)S(1)} %fusion.224), channel_id=1, source_target_pairs={{240,0},{0,16},{16,32},{32,48},{48,64},{64,80},{80,96},{96,112},{1... | collective-permute-start | bytes 1179656 | tf_op jit(solution)/shard_map/while/body/eval_jaxpr/ppermute | solution.py:25
  531.9 10.2 collective-permute-start
  568.6 13.4 %collective-permute-start.4 = (f32[3,2,128,128]{3,2,1,0:T(8,128)S(1)}, f32[3,2,128,128]{3,2,1,0:T(8,128)S(1)}, u32[]{:S(2)}, u32[]{:S(2)}) collective-permute-start(f32[3,2,128,128]{3,2,1,0:T(8,128)S(1)} %fusion.224), channel_id=1, source_target_pairs={{240,0},{0,16},{16,32},{32,48},{48,64},{64,80},{80,96},{96,112},{1... | collective-permute-start | bytes 1179656 | tf_op jit(solution)/shard_map/while/body/eval_jaxpr/ppermute | solution.py:25
  582.1 11.8 %collective-permute-start = (f32[2,1,128,128]{3,2,1,0:T(8,128)S(1)}, f32[2,1,128,128]{3,2,1,0:T(8,128)S(1)}, u32[]{:S(2)}, u32[]{:S(2)}) collective-permute-start(f32[2,1,128,128]{3,2,1,0:T(8,128)S(1)} %slice.3017), channel_id=1, source_target_pairs={{1,0},{2,1},{3,2},{4,3},{5,4},{6,5},{7,6},{8,7},{9,8},{10,9},{11,1... | collective-permute-start | bytes 393224 | tf_op jit(solution)/shard_map/while/body/eval_jaxpr/ppermute | solution.py:19
  620.4 13.4 %collective-permute-start.4 = (f32[3,2,128,128]{3,2,1,0:T(8,128)S(1)}, f32[3,2,128,128]{3,2,1,0:T(8,128)S(1)}, u32[]{:S(2)}, u32[]{:S(2)}) collective-permute-start(f32[3,2,128,128]{3,2,1,0:T(8,128)S(1)} %fusion.224), channel_id=1, source_target_pairs={{240,0},{0,16},{16,32},{32,48},{48,64},{64,80},{80,96},{96,112},{1... | collective-permute-start | bytes 1179656 | tf_op jit(solution)/shard_map/while/body/eval_jaxpr/ppermute | solution.py:25
  633.9 11.9 %collective-permute-start = (f32[2,1,128,128]{3,2,1,0:T(8,128)S(1)}, f32[2,1,128,128]{3,2,1,0:T(8,128)S(1)}, u32[]{:S(2)}, u32[]{:S(2)}) collective-permute-start(f32[2,1,128,128]{3,2,1,0:T(8,128)S(1)} %slice.3017), channel_id=1, source_target_pairs={{1,0},{2,1},{3,2},{4,3},{5,4},{6,5},{7,6},{8,7},{9,8},{10,9},{11,1... | collective-permute-start | bytes 393224 | tf_op jit(solution)/shard_map/while/body/eval_jaxpr/ppermute | solution.py:19
  672.3 13.4 %collective-permute-start.4 = (f32[3,2,128,128]{3,2,1,0:T(8,128)S(1)}, f32[3,2,128,128]{3,2,1,0:T(8,128)S(1)}, u32[]{:S(2)}, u32[]{:S(2)}) collective-permute-start(f32[3,2,128,128]{3,2,1,0:T(8,128)S(1)} %fusion.224), channel_id=1, source_target_pairs={{240,0},{0,16},{16,32},{32,48},{48,64},{64,80},{80,96},{96,112},{1... | collective-permute-start | bytes 1179656 | tf_op jit(solution)/shard_map/while/body/eval_jaxpr/ppermute | solution.py:25
  685.8 11.1 %collective-permute-start = (f32[2,1,128,128]{3,2,1,0:T(8,128)S(1)}, f32[2,1,128,128]{3,2,1,0:T(8,128)S(1)}, u32[]{:S(2)}, u32[]{:S(2)}) collective-permute-start(f32[2,1,128,128]{3,2,1,0:T(8,128)S(1)} %slice.3017), channel_id=1, source_target_pairs={{1,0},{2,1},{3,2},{4,3},{5,4},{6,5},{7,6},{8,7},{9,8},{10,9},{11,1... | collective-permute-start | bytes 393224 | tf_op jit(solution)/shard_map/while/body/eval_jaxpr/ppermute | solution.py:19
  723.4 13.4 %collective-permute-start.4 = (f32[3,2,128,128]{3,2,1,0:T(8,128)S(1)}, f32[3,2,128,128]{3,2,1,0:T(8,128)S(1)}, u32[]{:S(2)}, u32[]{:S(2)}) collective-permute-start(f32[3,2,128,128]{3,2,1,0:T(8,128)S(1)} %fusion.224), channel_id=1, source_target_pairs={{240,0},{0,16},{16,32},{32,48},{48,64},{64,80},{80,96},{96,112},{1... | collective-permute-start | bytes 1179656 | tf_op jit(solution)/shard_map/while/body/eval_jaxpr/ppermute | solution.py:25
  736.9 10.7 collective-permute-start
  774.1 13.4 %collective-permute-start.4 = (f32[3,2,128,128]{3,2,1,0:T(8,128)S(1)}, f32[3,2,128,128]{3,2,1,0:T(8,128)S(1)}, u32[]{:S(2)}, u32[]{:S(2)}) collective-permute-start(f32[3,2,128,128]{3,2,1,0:T(8,128)S(1)} %fusion.224), channel_id=1, source_target_pairs={{240,0},{0,16},{16,32},{32,48},{48,64},{64,80},{80,96},{96,112},{1... | collective-permute-start | bytes 1179656 | tf_op jit(solution)/shard_map/while/body/eval_jaxpr/ppermute | solution.py:25
  787.6 10.5 collective-permute-start
  824.5 13.4 %collective-permute-start.4 = (f32[3,2,128,128]{3,2,1,0:T(8,128)S(1)}, f32[3,2,128,128]{3,2,1,0:T(8,128)S(1)}, u32[]{:S(2)}, u32[]{:S(2)}) collective-permute-start(f32[3,2,128,128]{3,2,1,0:T(8,128)S(1)} %fusion.224), channel_id=1, source_target_pairs={{240,0},{0,16},{16,32},{32,48},{48,64},{64,80},{80,96},{96,112},{1... | collective-permute-start | bytes 1179656 | tf_op jit(solution)/shard_map/while/body/eval_jaxpr/ppermute | solution.py:25
  838.0 10.7 collective-permute-start
  875.1 13.4 %collective-permute-start.4 = (f32[3,2,128,128]{3,2,1,0:T(8,128)S(1)}, f32[3,2,128,128]{3,2,1,0:T(8,128)S(1)}, u32[]{:S(2)}, u32[]{:S(2)}) collective-permute-start(f32[3,2,128,128]{3,2,1,0:T(8,128)S(1)} %fusion.224), channel_id=1, source_target_pairs={{240,0},{0,16},{16,32},{32,48},{48,64},{64,80},{80,96},{96,112},{1... | collective-permute-start | bytes 1179656 | tf_op jit(solution)/shard_map/while/body/eval_jaxpr/ppermute | solution.py:25
  888.6 10.7 collective-permute-start
  925.8 13.4 %collective-permute-start.4 = (f32[3,2,128,128]{3,2,1,0:T(8,128)S(1)}, f32[3,2,128,128]{3,2,1,0:T(8,128)S(1)}, u32[]{:S(2)}, u32[]{:S(2)}) collective-permute-start(f32[3,2,128,128]{3,2,1,0:T(8,128)S(1)} %fusion.224), channel_id=1, source_target_pairs={{240,0},{0,16},{16,32},{32,48},{48,64},{64,80},{80,96},{96,112},{1... | collective-permute-start | bytes 1179656 | tf_op jit(solution)/shard_map/while/body/eval_jaxpr/ppermute | solution.py:25
  939.3 10.7 collective-permute-start
  976.4 13.4 %collective-permute-start.4 = (f32[3,2,128,128]{3,2,1,0:T(8,128)S(1)}, f32[3,2,128,128]{3,2,1,0:T(8,128)S(1)}, u32[]{:S(2)}, u32[]{:S(2)}) collective-permute-start(f32[3,2,128,128]{3,2,1,0:T(8,128)S(1)} %fusion.224), channel_id=1, source_target_pairs={{240,0},{0,16},{16,32},{32,48},{48,64},{64,80},{80,96},{96,112},{1... | collective-permute-start | bytes 1179656 | tf_op jit(solution)/shard_map/while/body/eval_jaxpr/ppermute | solution.py:25
  989.9 10.6 collective-permute-start
  1027.0 13.4 %collective-permute-start.4 = (f32[3,2,128,128]{3,2,1,0:T(8,128)S(1)}, f32[3,2,128,128]{3,2,1,0:T(8,128)S(1)}, u32[]{:S(2)}, u32[]{:S(2)}) collective-permute-start(f32[3,2,128,128]{3,2,1,0:T(8,128)S(1)} %fusion.224), channel_id=1, source_target_pairs={{240,0},{0,16},{16,32},{32,48},{48,64},{64,80},{80,96},{96,112},{1... | collective-permute-start | bytes 1179656 | tf_op jit(solution)/shard_map/while/body/eval_jaxpr/ppermute | solution.py:25
  1040.7 10.4 collective-permute-start.37
  (109 other events, 982.6 us)
where the time goes:
time: 1080 us
  waiting for transfers between devices  692 us (64%)
  starting transfers between devices  334 us (31%)
  other arithmetic  23.9 us (2%)
  local copies, waits for them, and re-layouts  21.5 us (2%)
    ppermute x96, waiting for transfers between devices, from_behind(): lax.ppermute(value, axis, [(source, source + steps) for source in range(f...  485 us
    ppermute x96, starting transfers between devices, from_behind(): lax.ppermute(value, axis, [(source, source + steps) for source in range(f...  333 us
    ppermute x15, waiting for transfers between devices, from_behind_2(): return lax.ppermute(block, axis, route)  207 us
  transfers between devices with their start and end apart: 111, of which 111 were waited for; matrix products, arithmetic and copies ran while one was open for 1% of the time, Pallas kernels for 0%

commit v1 on v0

v1 whole, which is shorter than its diff:
```python
import functools

import jax
import jax.numpy as jnp
from jax import lax
from jax.experimental import pallas as pl
from jax.experimental.pallas import tpu as pltpu
from jax.sharding import PartitionSpec as P

FSTEPS = 2
FSWEEPS = 8
CSWEEPS = 2

floor_rate = 0.05
top_rate = 1.0
curl_bound = 14.0

ROWS = 8


def chebyshev_weights(lower, upper, sweeps):
    theta, delta = 0.5 * (upper + lower), 0.5 * (upper - lower)
    sigma = theta / delta
    top = [1.0, sigma]
    for _ in range(sweeps):
        top.append(2.0 * sigma * top[-1] - top[-2])
    step = [1.0 / theta] + [0.0] * (sweeps - 1)
    weights = list(step)
    rho = 1.0 / sigma
    for k in range(1, sweeps):
        rho_next = 1.0 / (2.0 * sigma - rho)
        step = [rho_next * rho * v for v in step]
        step[k] += 2.0 * rho_next / delta / top[k]
        weights = [a + b for a, b in zip(weights, step)]
        rho = rho_next
    return theta, delta, weights, top[sweeps]


FINE = chebyshev_weights(FSTEPS * floor_rate, FSTEPS * top_rate + curl_bound, FSWEEPS)
COARSE = chebyshev_weights(floor_rate, top_rate + curl_bound, CSWEEPS)


def shifts(shape):
    rows, lanes = shape
    lane = lax.broadcasted_iota(jnp.int32, shape, 1)
    not_last, not_first = lane < lanes - 1, lane > 0

    def next_z(v):
        return jnp.where(not_last, pltpu.roll(v, lanes - 1, axis=1), 0.0)

    def prev_z(v):
        return jnp.where(not_first, pltpu.roll(v, 1, axis=1), 0.0)

    def next_y(v):
        return pltpu.roll(v, rows - 1, axis=0)

    def prev_y(v):
        return pltpu.roll(v, 1, axis=0)

    return next_z, prev_z, next_y, prev_y


def curl_sweep(field, rel, keep_top, emit, planes):
    rows = field.shape[2]
    next_z, prev_z, next_y, prev_y = shifts((rows, 128))

    def prev_y_in(v):
        w = prev_y(v)
        return jnp.concatenate((w[: rows - ROWS], w[rows - ROWS :] * keep_top), 0)

    def body(i, carry):
        hy_low, hz_low = carry
        ex, ey, ez = field[i, 0], field[i, 1], field[i, 2]
        ey_up, ez_up = field[i + 1, 1], field[i + 1, 2]
        nu = rel[i]
        hx = nu * ((next_y(ez) - ez) - (next_z(ey) - ey))
        hy = nu * ((next_z(ex) - ex) - (ez_up - ez))
        hz = nu * ((ey_up - ey) - (next_y(ex) - ex))
        kx = (prev_z(hy) - hy) - (prev_y_in(hz) - hz)
        ky = (hz_low - hz) - (prev_z(hx) - hx)
        kz = (prev_y_in(hx) - hx) - (hy_low - hy)
        emit(i, (ex, ey, ez), (kx, ky, kz))
        return hy, hz

    zero = jnp.zeros((rows, 128), jnp.float32)
    lax.fori_loop(0, planes, body, (zero, zero), unroll=2)


def load_rows(dst, low, own, high, blocks):
    def body(b, _):
        for j in range(2):
            for comp in range(3):
                dst[2 * b + j, comp, 0:ROWS] = low[b, comp, j]
                dst[2 * b + j, comp, ROWS : 2 * ROWS] = own[b, comp, j]
                dst[2 * b + j, comp, 2 * ROWS : 3 * ROWS] = high[b, comp, j]
        return 0

    lax.fori_loop(0, blocks, body, 0)
    for comp in range(3):
        dst[2 * blocks, comp] = jnp.zeros((3 * ROWS, 128), jnp.float32)


MID = slice(ROWS, 2 * ROWS)


def fine_kernel(first, flags, low, own, high, con, rel, *rest):
    if first:
        total, after, here, there, quot, nu2 = rest
    else:
        other, base, out, here, there, quot, nu2, total = rest
    blocks = own.shape[0]
    planes = 2 * blocks
    theta, delta, weights, scale = FINE
    keep_top = flags[0]
    load_rows(here, low, own, high, blocks)
    for comp in range(3):
        there[planes, comp] = jnp.zeros((3 * ROWS, 128), jnp.float32)

    def prepare(i, _):
        quot[i] = 2.0 * theta / delta - (2.0 * FSTEPS / delta) * con[i]
        nu2[i] = (2.0 / delta) * rel[i]
        return 0

    lax.fori_loop(0, planes, prepare, 0)

    buffers = (here, there)
    last = FSWEEPS if first else FSWEEPS - 1
    for k in range(last):
        now, new = buffers[k % 2], buffers[(k + 1) % 2]

        def emit(i, e, curl, k=k, new=new):
            b, j = i // 2, i % 2
            q = quot[i]
            for comp in range(3):
                v = q * e[comp] - curl[comp]
                if k == 0:
                    v = 0.5 * v
                    new[i, comp] = v
                    total[b, comp, j] = weights[0] * e[comp][MID] + weights[1] * v[MID]
                    continue
                if k + 1 < FSWEEPS:
                    v = v - new[i, comp]
                    new[i, comp] = v
                    acc = total[b, comp, j] + weights[k + 1] * v[MID]
                    if k + 1 == FSWEEPS - 1 and not first:
                        acc = base[b, comp, j] + flags[1] * (acc + other[b, comp, j])
                        out[b, comp, j] = acc
                    else:
                        total[b, comp, j] = acc
                else:
                    v = v[MID] - new[i, comp, MID]
                    mass = FSTEPS * con[i, MID]
                    after[b, comp, j] = (1.0 / scale) * v + mass * total[b, comp, j]

        curl_sweep(now, nu2, keep_top, emit, planes)


def coarse_kernel(count, flags, low, own, high, con, rel, out, state, curled, fac, nu3):
    blocks = own.shape[0]
    planes = 2 * blocks
    theta, delta, weights, _ = COARSE
    keep_top = flags[0]
    load_rows(state, low, own, high, blocks)
    for comp in range(3):
        curled[planes, comp] = jnp.zeros((3 * ROWS, 128), jnp.float32)

    def prepare(i, _):
        fac[i] = (weights[0] + weights[1] * theta / delta) - (weights[1] / delta) * con[i]
        nu3[i] = (weights[1] / delta) * rel[i]
        return 0

    lax.fori_loop(0, planes, prepare, 0)

    def one(final):
        def first(i, e, curl):
            for comp in range(3):
                curled[i, comp] = curl[comp]

        curl_sweep(state, rel, keep_top, first, planes)

        def second(i, u, curl):
            f = fac[i]
            for comp in range(3):
                v = state[i, comp] - f * u[comp] + curl[comp]
                if final:
                    out[i // 2, comp, i % 2] = v[MID]
                else:
                    state[i, comp] = v

        curl_sweep(curled, nu3, keep_top, second, planes)

    if count > 1:
        lax.fori_loop(0, count - 1, lambda n, z: (one(False), z)[1], 0)
    one(True)


def start_kernel(flags, state, old, src, begin, con, rel, state_up, state_low, src_up, src_low, rel_low, res, base, forced):
    planes = con.shape[0]
    ny = con.shape[1]
    theta, delta, weights, _ = COARSE
    next_z, prev_z, next_y, prev_y = shifts((ny, 128))
    row = lax.broadcasted_iota(jnp.int32, (ny, 128), 0)
    raw_next, raw_prev = next_y, prev_y

    def next_y(v):
        return jnp.where(row < ny - 1, raw_next(v), 0.0)

    def prev_y(v):
        return jnp.where(row > 0, raw_prev(v), 0.0)

    def curls(field, up, low):
        nu = rel_low[0]
        ex, ey, ez = low[0], low[1], low[2]
        hy_low = nu * ((next_z(ex) - ex) - (field[2, 0] - ez))
        hz_low = nu * ((field[1, 0] - ey) - (next_y(ex) - ex))
        for i in range(planes):
            ex, ey, ez = field[0, i], field[1, i], field[2, i]
            ey_up = field[1, i + 1] if i + 1 < planes else up[0]
            ez_up = field[2, i + 1] if i + 1 < planes else up[1]
            nu = rel[i]
            hx = nu * ((next_y(ez) - ez) - (next_z(ey) - ey))
            hy = nu * ((next_z(ex) - ex) - (ez_up - ez))
            hz = nu * ((ey_up - ey) - (next_y(ex) - ex))
            kx = (prev_z(hy) - hy) - (prev_y(hz) - hz)
            ky = (hz_low - hz) - (prev_z(hx) - hx)
            kz = (prev_y(hx) - hx) - (hy_low - hy)
            yield i, (ex, ey, ez), (kx, ky, kz)
            hy_low, hz_low = hy, hz

    def spread(ref, comp, i, v):
        for b in range(ny // ROWS):
            ref[b, comp, i] = v[b * ROWS : (b + 1) * ROWS]

    for i, e, curl in curls(state, state_up, state_low):
        for comp in range(3):
            spread(res, comp, i, src[comp, i] - curl[comp])
    for i, s, curl in curls(src, src_up, src_low):
        fac = (weights[0] + weights[1] * theta / delta) - (weights[1] / delta) * con[i]
        for comp in range(3):
            push = fac * s[comp] - (weights[1] / delta) * curl[comp]
            forced[comp, i] = push
            inner = state[comp, i] - old[comp, i] + push
            spread(base, comp, i, jnp.where(flags[1] > 0.0, inner, begin[comp, i]))


VMEM = pl.BlockSpec(memory_space=pltpu.VMEM)
SMEM = pl.BlockSpec(memory_space=pltpu.SMEM)


def call(kernel, name, outs, scratch, flags, *operands):
    return pl.pallas_call(
        kernel,
        name=name,
        out_shape=[jax.ShapeDtypeStruct(s, jnp.float32) for s in outs],
        in_specs=[SMEM] + [VMEM] * len(operands),
        out_specs=[VMEM] * len(outs),
        scratch_shapes=[pltpu.VMEM(s, jnp.float32) for s in scratch],
    )(flags, *operands)


def open_shift(value, steps):
    count = lax.axis_size("space")
    first, last = max(0, -steps), min(count, count - steps)
    return lax.ppermute(value, "space", [(i, i + steps) for i in range(first, last)])


def ring_shift(value, steps):
    count = lax.axis_size("slab")
    return lax.ppermute(value, "slab", [(i, (i + steps) % count) for i in range(count)])


def turn(value):
    return lax.all_to_all(value, "space", 0, 0, tiled=True)


def halo(value):
    return open_shift(value, 1), open_shift(value, -1)


def local(state_old, coarse_old, source, start_state, conduct, reluct, converged):
    groups = lax.axis_size("slab")
    spaces = lax.axis_size("space")
    position = (lax.axis_index("slab") - converged[0] % groups - 1) % groups
    turnpos = (position + 1) % groups
    inner = lax.axis_index("space") < spaces - 1
    flags = jnp.stack((inner, turnpos > 0)).astype(jnp.float32)
    state, src = state_old[0], source[0]
    planes, ny = conduct.shape[0], conduct.shape[1]
    blocks = spaces
    field = (blocks, 3, planes, ROWS, 128)
    nx = blocks * planes

    ups = open_shift(jnp.stack((state[1:3, 0], src[1:3, 0])), -1)
    lows = open_shift(jnp.concatenate((state[:, -1], src[:, -1], reluct[-1:])), 1)
    coef = jnp.stack((conduct, reluct)).reshape(2, planes, blocks, ROWS, 128).transpose(2, 0, 1, 3, 4)
    coef = turn(coef)
    coef_low, coef_high = halo(coef)
    coef24 = jnp.concatenate((coef_low, coef, coef_high), 3).transpose(1, 0, 2, 3, 4).reshape(2, nx, 3 * ROWS, 128)
    con, rel = coef24[0], coef24[1]

    res, base, forced = call(
        start_kernel, "start", [field, field, state.shape], [], flags,
        state, coarse_old[0], src, start_state, conduct, reluct,
        ups[0], lows[0:3], ups[1], lows[3:6], lows[6:7],
    )
    res = turn(res)
    res_low, res_high = halo(res)
    base = turn(base)

    wide = (nx + 1, 3, 3 * ROWS, 128)
    slim = (nx, 3 * ROWS, 128)
    total, after = call(
        functools.partial(fine_kernel, True), "fine_first", [field, field], [wide, wide, slim, slim], flags,
        res_low, res, res_high, con, rel,
    )
    after_low, after_high = halo(after)
    (lead,) = call(
        functools.partial(fine_kernel, False), "fine_second", [field], [wide, wide, slim, slim, field], flags,
        after_low, after, after_high, con, rel, total, base,
    )

    def coarse(value, count):
        low, high = halo(value)
        return call(
            functools.partial(coarse_kernel, count), "coarse%d" % count, [field], [wide, wide, slim, slim], flags,
            low, value, high, con, rel,
        )[0]

    def masked(value, condition):
        return jnp.where(condition, value, 0.0)

    lead = lead + masked(ring_shift(coarse(lead, 1), 1), turnpos >= 1)
    lead = lead + masked(ring_shift(coarse(lead, 2), 2), turnpos >= 2)
    chained = ring_shift(lead, 1)
    power = lead
    for step in range(4, groups, 4):
        power = coarse(power, 4)
        chained = chained + masked(ring_shift(power, step + 1), position >= step)
    moved = coarse(chained, 1)

    def home(value):
        return turn(value).transpose(1, 2, 0, 3, 4).reshape(3, planes, ny, 128)

    return home(chained)[None], (home(moved) + forced)[None]


def solution(mesh):
    placed = (
        P("slab", None, "space", None, None),
        P("slab", None, "space", None, None),
        P("slab", None, "space", None, None),
        P(None, "space", None, None),
        P("space", None, None),
        P("space", None, None),
        P(),
    )
    return jax.shard_map(
        local,
        mesh=mesh,
        in_specs=placed,
        out_specs=(P("slab", None, "space", None, None), P("slab", None, "space", None, None)),
        check_vma=False,
    )
```

time: 1080 us -> 409 us (0.38)
  the two profiles are of different devices: /device:TPU:160 before, /device:TPU:1 now
where the time goes in v1:
time: 409 us; the launch traced here: 407 us
  starting transfers between devices  181 us (44%)
  Pallas kernels  142 us (35%)
  waiting for transfers between devices  64.8 us (16%)
  local copies, waits for them, and re-layouts  13.7 us (3%)
    pallas_call x9, Pallas kernels, call(): pl.pallas_call(kernel, name=name, out_shape=[jax.ShapeDtypeStruct(s, jnp....  142 us
    ppermute x20, starting transfers between devices, open_shift(): lax.ppermute(value, 'space', [(i, i + steps) for i in range(first, last)])  73 us
    all_to_all x5, starting transfers between devices, turn(): return lax.all_to_all(value, 'space', 0, 0, tiled=True)  70.4 us
    ppermute x6, starting transfers between devices, ring_shift(): lax.ppermute(value, 'slab', [(i, (i + steps) % count) for i in range(coun...  37.9 us
    ppermute x20, waiting for transfers between devices, open_shift(): lax.ppermute(value, 'space', [(i, i + steps) for i in range(first, last)])  29.3 us
    ppermute x6, waiting for transfers between devices, ring_shift(): lax.ppermute(value, 'slab', [(i, (i + steps) % count) for i in range(coun...  19.2 us
    all_to_all x5, waiting for transfers between devices, turn(): return lax.all_to_all(value, 'space', 0, 0, tiled=True)  16.2 us
    unnamed x56, local copies, waits for them, and re-layouts  8.22 us
  transfers between devices with their start and end apart: 31, of which 18 were waited for; matrix products, arithmetic and copies ran while one was open for 1% of the time, Pallas kernels for 14%

profile of v1, /device:TPU:1, one launch (start us, length us, event | category | flops | bytes accessed | tf_op | source)
XLA Modules:
  0.0 407.3 jit_solution(11986132719108141089)
XLA Ops:
  4.1 4.8 %collective-permute-start.1 = (f32[7,128,128]{2,1,0:T(8,128)S(1)}, f32[7,128,128]{2,1,0:T(8,128)S(1)}, u32[]{:S(2)}, u32[]{:S(2)}) collective-permute-start(f32[7,128,128]{2,1,0:T(8,128)S(1)} %pad_maximum_fusion), channel_id=1, source_target_pairs={{0,1},{1,2},{2,3},{3,4},{4,5},{5,6},{6,7},{7,8},{8,9},{9,10},{10,1... | collective-permute-start | bytes 1376264 | tf_op jit(solution)/shard_map/ppermute | solution.py:264
  9.6 9.1 %all-to-all-start.1 = ((f32[16,2,2,8,128]{4,3,2,1,0:T(8,128)}), f32[16,2,2,8,128]{4,3,2,1,0:T(8,128)S(1)}, u32[]{:S(2)}, u32[]{:S(2)}) async-start(f32[16,2,2,8,128]{4,3,2,1,0:T(8,128)} %copy.33), calls=%async_computation.1 | async-start | bytes 524288 | tf_op jit(solution)/shard_map/all_to_all | solution.py:273
  27.7 6.5 %all-to-all-start = ((f32[16,3,2,8,128]{4,3,2,1,0:T(8,128)}), f32[16,3,2,8,128]{4,3,2,1,0:T(8,128)S(1)}, u32[]{:S(2)}, u32[]{:S(2)}) async-start(f32[16,3,2,8,128]{4,3,2,1,0:T(8,128)} %get-tuple-element.7), calls=%async_computation | async-start | bytes 786432 | tf_op jit(solution)/shard_map/all_to_all | solution.py:273
  39.5 4.7 %all-to-all-done.own = f32[16,3,2,8,128]{4,3,2,1,0:T(8,128)S(1)} async-done(((f32[16,3,2,8,128]{4,3,2,1,0:T(8,128)}), f32[16,3,2,8,128]{4,3,2,1,0:T(8,128)S(1)}, u32[]{:S(2)}, u32[]{:S(2)}) %all-to-all-start) | async-done | bytes 393248 | tf_op jit(solution)/shard_map/all_to_all | solution.py:273
  45.5 4.0 collective-permute-start.2
  49.5 5.3 %all-to-all-start.2 = ((f32[16,3,2,8,128]{4,3,2,1,0:T(8,128)}), f32[16,3,2,8,128]{4,3,2,1,0:T(8,128)S(1)}, u32[]{:S(2)}, u32[]{:S(2)}) async-start(f32[16,3,2,8,128]{4,3,2,1,0:T(8,128)} %get-tuple-element.10), calls=%async_computation.2 | async-start | bytes 786432 | tf_op jit(solution)/shard_map/all_to_all | solution.py:273
  56.7 22.8 %fine_first.1 = (f32[16,3,2,8,128]{4,3,2,1,0:T(8,128)}, f32[16,3,2,8,128]{4,3,2,1,0:T(8,128)}) custom-call(f32[2]{0:T(128)} %add_convert_fusion.flags, f32[16,3,2,8,128]{4,3,2,1,0:T(8,128)} %copy-done.24, f32[16,3,2,8,128]{4,3,2,1,0:T(8,128)} %copy-done.5, f32[16,3,2,8,128]{4,3,2,1,0:T(8,128)} %copy-done.23, f32[32,24,128]{2,1,0:T(8,128)} %bitcast.57, ...), custom_call_target="tpu_custom_call" | custom-call | tf_op jit(solution)/shard_map/fine_first/pallas_call | solution.py:251
  80.8 4.0 collective-permute-start.6
  90.5 20.6 %fine_second.1.own = f32[16,3,2,8,128]{4,3,2,1,0:T(8,128)} custom-call(f32[2]{0:T(128)} %add_convert_fusion.flags, f32[16,3,2,8,128]{4,3,2,1,0:T(8,128)} %copy-done.26, f32[16,3,2,8,128]{4,3,2,1,0:T(8,128)} %get-tuple-element.8.own, f32[16,3,2,8,128]{4,3,2,1,0:T(8,128)} %copy-done.25, f32[32,24,128]{2,1,0:T(8,128)} %bitcast.58, f32[32,24,128]{2,1,0:T(8,128)} %bitcast.50, ...), custom_call_target="tpu_custom_call" | custom-call | tf_op jit(solution)/shard_map/fine_second/pallas_call | solution.py:251
  112.5 4.4 %collective-permute-start.8 = (f32[16,3,2,8,128]{4,3,2,1,0:T(8,128)}, f32[16,3,2,8,128]{4,3,2,1,0:T(8,128)S(1)}, u32[]{:S(2)}, u32[]{:S(2)}) collective-permute-start(f32[16,3,2,8,128]{4,3,2,1,0:T(8,128)} %fine_second.1.own), channel_id=1, source_target_pairs={{0,1},{1,2},{2,3},{3,4},{4,5},{5,6},{6,7},{7,8},{8,9},{9,10},{10,1... | collective-permute-start | bytes 1179656 | tf_op jit(solution)/shard_map/ppermute | solution.py:264
  122.6 7.5 %coarse1.2 = f32[16,3,2,8,128]{4,3,2,1,0:T(8,128)} custom-call(f32[2]{0:T(128)} %add_convert_fusion.flags, f32[16,3,2,8,128]{4,3,2,1,0:T(8,128)} %copy-done.18, f32[16,3,2,8,128]{4,3,2,1,0:T(8,128)} %fine_second.1.own, f32[16,3,2,8,128]{4,3,2,1,0:T(8,128)} %copy-done.13, f32[32,24,128]{2,1,0:T(8,128)} %bitcast.59, f32[32,24,128]{2,1,0:T(8,128)} %bitcast.51), custom_call_target="tpu_custom_call" | custom-call | tf_op jit(solution)/shard_map/coarse1/pallas_call | solution.py:251
  130.1 10.1 %collective-permute-start.10 = (f32[16,3,2,8,128]{4,3,2,1,0:T(8,128)}, f32[16,3,2,8,128]{4,3,2,1,0:T(8,128)S(1)}, u32[]{:S(2)}, u32[]{:S(2)}) collective-permute-start(f32[16,3,2,8,128]{4,3,2,1,0:T(8,128)} %coarse1.2), channel_id=1, source_target_pairs={{0,16},{16,32},{32,48},{48,64},{64,80},{80,96},{96,112},{112,128},... | collective-permute-start | bytes 1179656 | tf_op jit(solution)/shard_map/ppermute | solution.py:269
  140.2 5.0 %collective-permute-done.10 = f32[16,3,2,8,128]{4,3,2,1,0:T(8,128)S(1)} collective-permute-done((f32[16,3,2,8,128]{4,3,2,1,0:T(8,128)}, f32[16,3,2,8,128]{4,3,2,1,0:T(8,128)S(1)}, u32[]{:S(2)}, u32[]{:S(2)}) %collective-permute-start.10) | collective-permute-done | bytes 393248 | tf_op jit(solution)/shard_map/ppermute | solution.py:269
  146.6 4.7 %collective-permute-start.11 = (f32[16,3,2,8,128]{4,3,2,1,0:T(8,128)S(1)}, f32[16,3,2,8,128]{4,3,2,1,0:T(8,128)S(1)}, u32[]{:S(2)}, u32[]{:S(2)}) collective-permute-start(f32[16,3,2,8,128]{4,3,2,1,0:T(8,128)S(1)} %select_add_fusion.2.own), channel_id=1, source_target_pairs={{0,1},{1,2},{2,3},{3,4},{4,5},{5,6},{6,7},{7,8},{8,9},{9,10},{10,1... | collective-permute-start | bytes 1179656 | tf_op jit(solution)/shard_map/ppermute | solution.py:264
  156.7 12.5 %coarse2.1 = f32[16,3,2,8,128]{4,3,2,1,0:T(8,128)} custom-call(f32[2]{0:T(128)} %add_convert_fusion.flags, f32[16,3,2,8,128]{4,3,2,1,0:T(8,128)} %copy-done.19, f32[16,3,2,8,128]{4,3,2,1,0:T(8,128)} %copy-done, f32[16,3,2,8,128]{4,3,2,1,0:T(8,128)} %copy-done.14, f32[32,24,128]{2,1,0:T(8,128)} %bitcast.60, f32[32,24,128]{2,1,0:T(8,128)} %bitcast.52), custom_call_target="tpu_custom_call" | custom-call | tf_op jit(solution)/shard_map/coarse2/pallas_call | solution.py:251
  173.0 9.2 %collective-permute-done.13 = f32[16,3,2,8,128]{4,3,2,1,0:T(8,128)S(1)} collective-permute-done((f32[16,3,2,8,128]{4,3,2,1,0:T(8,128)}, f32[16,3,2,8,128]{4,3,2,1,0:T(8,128)S(1)}, u32[]{:S(2)}, u32[]{:S(2)}) %collective-permute-start.13) | collective-permute-done | bytes 393248 | tf_op jit(solution)/shard_map/ppermute | solution.py:269
  184.5 5.2 %collective-permute-start.15 = (f32[16,3,2,8,128]{4,3,2,1,0:T(8,128)S(1)}, f32[16,3,2,8,128]{4,3,2,1,0:T(8,128)S(1)}, u32[]{:S(2)}, u32[]{:S(2)}) collective-permute-start(f32[16,3,2,8,128]{4,3,2,1,0:T(8,128)S(1)} %select_add_fusion.1.own), channel_id=1, source_target_pairs={{0,1},{1,2},{2,3},{3,4},{4,5},{5,6},{6,7},{7,8},{8,9},{9,10},{10,1... | collective-permute-start | bytes 1179656 | tf_op jit(solution)/shard_map/ppermute | solution.py:264
  195.1 22.7 %coarse4.3.own = f32[16,3,2,8,128]{4,3,2,1,0:T(8,128)} custom-call(f32[2]{0:T(128)} %add_convert_fusion.flags, f32[16,3,2,8,128]{4,3,2,1,0:T(8,128)} %copy-done.20, f32[16,3,2,8,128]{4,3,2,1,0:T(8,128)} %copy-done.3, f32[16,3,2,8,128]{4,3,2,1,0:T(8,128)} %copy-done.15, f32[32,24,128]{2,1,0:T(8,128)} %bitcast.61, f32[32,24,128]{2,1,0:T(8,128)} %bitcast.53), custom_call_target="tpu_custom_call" | custom-call | tf_op jit(solution)/shard_map/coarse4/pallas_call | solution.py:251
  219.2 6.8 %collective-permute-start.18 = (f32[16,3,2,8,128]{4,3,2,1,0:T(8,128)}, f32[16,3,2,8,128]{4,3,2,1,0:T(8,128)S(1)}, u32[]{:S(2)}, u32[]{:S(2)}) collective-permute-start(f32[16,3,2,8,128]{4,3,2,1,0:T(8,128)} %coarse4.3.own), channel_id=1, source_target_pairs={{0,1},{1,2},{2,3},{3,4},{4,5},{5,6},{6,7},{7,8},{8,9},{9,10},{10,1... | collective-permute-start | bytes 1179656 | tf_op jit(solution)/shard_map/ppermute | solution.py:264
  231.7 22.7 %coarse4.4.own = f32[16,3,2,8,128]{4,3,2,1,0:T(8,128)} custom-call(f32[2]{0:T(128)} %add_convert_fusion.flags, f32[16,3,2,8,128]{4,3,2,1,0:T(8,128)} %copy-done.21, f32[16,3,2,8,128]{4,3,2,1,0:T(8,128)} %coarse4.3.own, f32[16,3,2,8,128]{4,3,2,1,0:T(8,128)} %copy-done.16, f32[32,24,128]{2,1,0:T(8,128)} %bitcast.62, f32[32,24,128]{2,1,0:T(8,128)} %bitcast.54), custom_call_target="tpu_custom_call" | custom-call | tf_op jit(solution)/shard_map/coarse4/pallas_call | solution.py:251
  255.8 18.2 %collective-permute-start.21 = (f32[16,3,2,8,128]{4,3,2,1,0:T(8,128)}, f32[16,3,2,8,128]{4,3,2,1,0:T(8,128)S(1)}, u32[]{:S(2)}, u32[]{:S(2)}) collective-permute-start(f32[16,3,2,8,128]{4,3,2,1,0:T(8,128)} %coarse4.4.own), channel_id=1, source_target_pairs={{0,1},{1,2},{2,3},{3,4},{4,5},{5,6},{6,7},{7,8},{8,9},{9,10},{10,1... | collective-permute-start | bytes 1179656 | tf_op jit(solution)/shard_map/ppermute | solution.py:264
  274.0 10.6 %collective-permute-start.17 = (f32[16,3,2,8,128]{4,3,2,1,0:T(8,128)S(1)}, f32[16,3,2,8,128]{4,3,2,1,0:T(8,128)S(1)}, u32[]{:S(2)}, u32[]{:S(2)}) collective-permute-start(f32[16,3,2,8,128]{4,3,2,1,0:T(8,128)S(1)} %copy-done.2), channel_id=1, source_target_pairs={{0,80},{16,96},{32,112},{48,128},{64,144},{80,160},{96,176},{112,1... | collective-permute-start | bytes 1179656 | tf_op jit(solution)/shard_map/ppermute | solution.py:269
  284.7 5.9 %collective-permute-start.20 = (f32[16,3,2,8,128]{4,3,2,1,0:T(8,128)}, f32[16,3,2,8,128]{4,3,2,1,0:T(8,128)S(1)}, u32[]{:S(2)}, u32[]{:S(2)}) collective-permute-start(f32[16,3,2,8,128]{4,3,2,1,0:T(8,128)} %coarse4.4.own), channel_id=1, source_target_pairs={{0,144},{16,160},{32,176},{48,192},{64,208},{80,224},{96,240},{112... | collective-permute-start | bytes 1179656 | tf_op jit(solution)/shard_map/ppermute | solution.py:269
  292.0 22.7 %coarse4.5 = f32[16,3,2,8,128]{4,3,2,1,0:T(8,128)} custom-call(f32[2]{0:T(128)} %add_convert_fusion.flags, f32[16,3,2,8,128]{4,3,2,1,0:T(8,128)} %copy-done.11, f32[16,3,2,8,128]{4,3,2,1,0:T(8,128)} %coarse4.4.own, f32[16,3,2,8,128]{4,3,2,1,0:T(8,128)} %copy-done.10, f32[32,24,128]{2,1,0:T(8,128)} %bitcast.63, f32[32,24,128]{2,1,0:T(8,128)} %bitcast.55), custom_call_target="tpu_custom_call" | custom-call | tf_op jit(solution)/shard_map/coarse4/pallas_call | solution.py:251
  314.8 7.5 %collective-permute-start.23 = (f32[16,3,2,8,128]{4,3,2,1,0:T(8,128)}, f32[16,3,2,8,128]{4,3,2,1,0:T(8,128)S(1)}, u32[]{:S(2)}, u32[]{:S(2)}) collective-permute-start(f32[16,3,2,8,128]{4,3,2,1,0:T(8,128)} %coarse4.5), channel_id=1, source_target_pairs={{0,208},{16,224},{32,240},{48,0},{64,16},{80,32},{96,48},{112,64},... | collective-permute-start | bytes 1179656 | tf_op jit(solution)/shard_map/ppermute | solution.py:269
  322.3 5.0 %collective-permute-done.23 = f32[16,3,2,8,128]{4,3,2,1,0:T(8,128)S(1)} collective-permute-done((f32[16,3,2,8,128]{4,3,2,1,0:T(8,128)}, f32[16,3,2,8,128]{4,3,2,1,0:T(8,128)S(1)}, u32[]{:S(2)}, u32[]{:S(2)}) %collective-permute-start.23) | collective-permute-done | bytes 393248 | tf_op jit(solution)/shard_map/ppermute | solution.py:269
  328.2 37.5 %all-to-all-start.3 = ((f32[16,3,2,8,128]{4,3,2,1,0:T(8,128)}), f32[16,3,2,8,128]{4,3,2,1,0:T(8,128)S(1)}, u32[]{:S(2)}, u32[]{:S(2)}) async-start(f32[16,3,2,8,128]{4,3,2,1,0:T(8,128)} %select_add_fusion.own), calls=%async_computation.3 | async-start | bytes 786432 | tf_op jit(solution)/shard_map/all_to_all | solution.py:273
  366.9 4.0 collective-permute-start.24
  371.0 4.5 %collective-permute-done.25.high = f32[16,3,2,8,128]{4,3,2,1,0:T(8,128)S(1)} collective-permute-done((f32[16,3,2,8,128]{4,3,2,1,0:T(8,128)}, f32[16,3,2,8,128]{4,3,2,1,0:T(8,128)S(1)}, u32[]{:S(2)}, u32[]{:S(2)}) %collective-permute-start.25) | collective-permute-done | bytes 393248 | tf_op jit(solution)/shard_map/ppermute | solution.py:264
  376.9 7.5 %coarse1.3 = f32[16,3,2,8,128]{4,3,2,1,0:T(8,128)} custom-call(f32[2]{0:T(128)} %add_convert_fusion.flags, f32[16,3,2,8,128]{4,3,2,1,0:T(8,128)} %copy-done.17, f32[16,3,2,8,128]{4,3,2,1,0:T(8,128)} %select_add_fusion.own, f32[16,3,2,8,128]{4,3,2,1,0:T(8,128)} %copy-done.12, f32[32,24,128]{2,1,0:T(8,128)} %bitcast.64, f32[32,24,128]{2,1,0:T(8,128)} %bitcast.56), custom_call_target="tpu_custom_call" | custom-call | tf_op jit(solution)/shard_map/coarse1/pallas_call | solution.py:251
  384.4 12.1 %all-to-all-start.4 = ((f32[16,3,2,8,128]{4,3,2,1,0:T(8,128)}), f32[16,3,2,8,128]{4,3,2,1,0:T(8,128)S(1)}, u32[]{:S(2)}, u32[]{:S(2)}) async-start(f32[16,3,2,8,128]{4,3,2,1,0:T(8,128)} %coarse1.3), calls=%async_computation.4 | async-start | bytes 786432 | tf_op jit(solution)/shard_map/all_to_all | solution.py:273
  397.3 9.2 %all-to-all-done.4 = f32[16,3,2,8,128]{4,3,2,1,0:T(8,128)S(1)} async-done(((f32[16,3,2,8,128]{4,3,2,1,0:T(8,128)}), f32[16,3,2,8,128]{4,3,2,1,0:T(8,128)S(1)}, u32[]{:S(2)}, u32[]{:S(2)}) %all-to-all-start.4) | async-done | bytes 393248 | tf_op jit(solution)/shard_map/all_to_all | solution.py:273
  (114 shorter events, 68.4 us)
Async XLA Ops:
  1.8 18.2 %collective-permute-start = (f32[2,2,128,128]{3,2,1,0:T(8,128)S(1)}, f32[2,2,128,128]{3,2,1,0:T(8,128)S(1)}, u32[]{:S(2)}, u32[]{:S(2)}) collective-permute-start(f32[2,2,128,128]{3,2,1,0:T(8,128)S(1)} %pad_maximum_fusion.1), channel_id=1, source_target_pairs={{1,0},{2,1},{3,2},{4,3},{5,4},{6,5},{7,6},{8,7},{9,8},{10,9},{11,1... | collective-permute-start | bytes 786440 | tf_op jit(solution)/shard_map/ppermute | solution.py:264
  4.1 16.7 %collective-permute-start.1 = (f32[7,128,128]{2,1,0:T(8,128)S(1)}, f32[7,128,128]{2,1,0:T(8,128)S(1)}, u32[]{:S(2)}, u32[]{:S(2)}) collective-permute-start(f32[7,128,128]{2,1,0:T(8,128)S(1)} %pad_maximum_fusion), channel_id=1, source_target_pairs={{0,1},{1,2},{2,3},{3,4},{4,5},{5,6},{6,7},{7,8},{8,9},{9,10},{10,1... | collective-permute-start | bytes 1376264 | tf_op jit(solution)/shard_map/ppermute | solution.py:264
  9.6 18.0 %all-to-all-start.1 = ((f32[16,2,2,8,128]{4,3,2,1,0:T(8,128)}), f32[16,2,2,8,128]{4,3,2,1,0:T(8,128)S(1)}, u32[]{:S(2)}, u32[]{:S(2)}) async-start(f32[16,2,2,8,128]{4,3,2,1,0:T(8,128)} %copy.33), calls=%async_computation.1 | async-start | bytes 524288 | tf_op jit(solution)/shard_map/all_to_all | solution.py:273
  27.7 16.5 %all-to-all-start = ((f32[16,3,2,8,128]{4,3,2,1,0:T(8,128)}), f32[16,3,2,8,128]{4,3,2,1,0:T(8,128)S(1)}, u32[]{:S(2)}, u32[]{:S(2)}) async-start(f32[16,3,2,8,128]{4,3,2,1,0:T(8,128)} %get-tuple-element.7), calls=%async_computation | async-start | bytes 786432 | tf_op jit(solution)/shard_map/all_to_all | solution.py:273
  34.2 20.6 %collective-permute-start.5 = (f32[16,2,2,8,128]{4,3,2,1,0:T(8,128)S(1)}, f32[16,2,2,8,128]{4,3,2,1,0:T(8,128)S(1)}, u32[]{:S(2)}, u32[]{:S(2)}) collective-permute-start(f32[16,2,2,8,128]{4,3,2,1,0:T(8,128)S(1)} %all-to-all-done.1), channel_id=1, source_target_pairs={{1,0},{2,1},{3,2},{4,3},{5,4},{6,5},{7,6},{8,7},{9,8},{10,9},{11,1... | collective-permute-start | bytes 786440 | tf_op jit(solution)/shard_map/ppermute | solution.py:264
  35.5 19.3 %collective-permute-start.4 = (f32[16,2,2,8,128]{4,3,2,1,0:T(8,128)S(1)}, f32[16,2,2,8,128]{4,3,2,1,0:T(8,128)S(1)}, u32[]{:S(2)}, u32[]{:S(2)}) collective-permute-start(f32[16,2,2,8,128]{4,3,2,1,0:T(8,128)S(1)} %all-to-all-done.1), channel_id=1, source_target_pairs={{0,1},{1,2},{2,3},{3,4},{4,5},{5,6},{6,7},{7,8},{8,9},{9,10},{10,1... | collective-permute-start | bytes 786440 | tf_op jit(solution)/shard_map/ppermute | solution.py:264
  44.2 11.6 %collective-permute-start.3 = (f32[16,3,2,8,128]{4,3,2,1,0:T(8,128)S(1)}, f32[16,3,2,8,128]{4,3,2,1,0:T(8,128)S(1)}, u32[]{:S(2)}, u32[]{:S(2)}) collective-permute-start(f32[16,3,2,8,128]{4,3,2,1,0:T(8,128)S(1)} %all-to-all-done.own), channel_id=1, source_target_pairs={{1,0},{2,1},{3,2},{4,3},{5,4},{6,5},{7,6},{8,7},{9,8},{10,9},{11,1... | collective-permute-start | bytes 1179656 | tf_op jit(solution)/shard_map/ppermute | solution.py:264
  45.5 10.4 %collective-permute-start.2 = (f32[16,3,2,8,128]{4,3,2,1,0:T(8,128)S(1)}, f32[16,3,2,8,128]{4,3,2,1,0:T(8,128)S(1)}, u32[]{:S(2)}, u32[]{:S(2)}) collective-permute-start(f32[16,3,2,8,128]{4,3,2,1,0:T(8,128)S(1)} %all-to-all-done.own), channel_id=1, source_target_pairs={{0,1},{1,2},{2,3},{3,4},{4,5},{5,6},{6,7},{7,8},{8,9},{9,10},{10,1... | collective-permute-start | bytes 1179656 | tf_op jit(solution)/shard_map/ppermute | solution.py:264
  49.5 35.3 %all-to-all-start.2 = ((f32[16,3,2,8,128]{4,3,2,1,0:T(8,128)}), f32[16,3,2,8,128]{4,3,2,1,0:T(8,128)S(1)}, u32[]{:S(2)}, u32[]{:S(2)}) async-start(f32[16,3,2,8,128]{4,3,2,1,0:T(8,128)} %get-tuple-element.10), calls=%async_computation.2 | async-start | bytes 786432 | tf_op jit(solution)/shard_map/all_to_all | solution.py:273
  79.5 8.7 %collective-permute-start.7 = (f32[16,3,2,8,128]{4,3,2,1,0:T(8,128)}, f32[16,3,2,8,128]{4,3,2,1,0:T(8,128)S(1)}, u32[]{:S(2)}, u32[]{:S(2)}) collective-permute-start(f32[16,3,2,8,128]{4,3,2,1,0:T(8,128)} %get-tuple-element.8.own), channel_id=1, source_target_pairs={{1,0},{2,1},{3,2},{4,3},{5,4},{6,5},{7,6},{8,7},{9,8},{10,9},{11,1... | collective-permute-start | bytes 1179656 | tf_op jit(solution)/shard_map/ppermute | solution.py:264
  80.8 9.0 %collective-permute-start.6 = (f32[16,3,2,8,128]{4,3,2,1,0:T(8,128)}, f32[16,3,2,8,128]{4,3,2,1,0:T(8,128)S(1)}, u32[]{:S(2)}, u32[]{:S(2)}) collective-permute-start(f32[16,3,2,8,128]{4,3,2,1,0:T(8,128)} %get-tuple-element.8.own), channel_id=1, source_target_pairs={{0,1},{1,2},{2,3},{3,4},{4,5},{5,6},{6,7},{7,8},{8,9},{9,10},{10,1... | collective-permute-start | bytes 1179656 | tf_op jit(solution)/shard_map/ppermute | solution.py:264
  111.1 9.2 %collective-permute-start.9 = (f32[16,3,2,8,128]{4,3,2,1,0:T(8,128)}, f32[16,3,2,8,128]{4,3,2,1,0:T(8,128)S(1)}, u32[]{:S(2)}, u32[]{:S(2)}) collective-permute-start(f32[16,3,2,8,128]{4,3,2,1,0:T(8,128)} %fine_second.1.own), channel_id=1, source_target_pairs={{1,0},{2,1},{3,2},{4,3},{5,4},{6,5},{7,6},{8,7},{9,8},{10,9},{11,1... | collective-permute-start | bytes 1179656 | tf_op jit(solution)/shard_map/ppermute | solution.py:264
  112.5 9.4 %collective-permute-start.8 = (f32[16,3,2,8,128]{4,3,2,1,0:T(8,128)}, f32[16,3,2,8,128]{4,3,2,1,0:T(8,128)S(1)}, u32[]{:S(2)}, u32[]{:S(2)}) collective-permute-start(f32[16,3,2,8,128]{4,3,2,1,0:T(8,128)} %fine_second.1.own), channel_id=1, source_target_pairs={{0,1},{1,2},{2,3},{3,4},{4,5},{5,6},{6,7},{7,8},{8,9},{9,10},{10,1... | collective-permute-start | bytes 1179656 | tf_op jit(solution)/shard_map/ppermute | solution.py:264
  130.1 15.2 %collective-permute-start.10 = (f32[16,3,2,8,128]{4,3,2,1,0:T(8,128)}, f32[16,3,2,8,128]{4,3,2,1,0:T(8,128)S(1)}, u32[]{:S(2)}, u32[]{:S(2)}) collective-permute-start(f32[16,3,2,8,128]{4,3,2,1,0:T(8,128)} %coarse1.2), channel_id=1, source_target_pairs={{0,16},{16,32},{32,48},{48,64},{64,80},{80,96},{96,112},{112,128},... | collective-permute-start | bytes 1179656 | tf_op jit(solution)/shard_map/ppermute | solution.py:269
  145.3 9.2 %collective-permute-start.12 = (f32[16,3,2,8,128]{4,3,2,1,0:T(8,128)S(1)}, f32[16,3,2,8,128]{4,3,2,1,0:T(8,128)S(1)}, u32[]{:S(2)}, u32[]{:S(2)}) collective-permute-start(f32[16,3,2,8,128]{4,3,2,1,0:T(8,128)S(1)} %select_add_fusion.2.own), channel_id=1, source_target_pairs={{1,0},{2,1},{3,2},{4,3},{5,4},{6,5},{7,6},{8,7},{9,8},{10,9},{11,1... | collective-permute-start | bytes 1179656 | tf_op jit(solution)/shard_map/ppermute | solution.py:264
  146.6 9.3 %collective-permute-start.11 = (f32[16,3,2,8,128]{4,3,2,1,0:T(8,128)S(1)}, f32[16,3,2,8,128]{4,3,2,1,0:T(8,128)S(1)}, u32[]{:S(2)}, u32[]{:S(2)}) collective-permute-start(f32[16,3,2,8,128]{4,3,2,1,0:T(8,128)S(1)} %select_add_fusion.2.own), channel_id=1, source_target_pairs={{0,1},{1,2},{2,3},{3,4},{4,5},{5,6},{6,7},{7,8},{8,9},{9,10},{10,1... | collective-permute-start | bytes 1179656 | tf_op jit(solution)/shard_map/ppermute | solution.py:264
  169.3 12.9 %collective-permute-start.13 = (f32[16,3,2,8,128]{4,3,2,1,0:T(8,128)}, f32[16,3,2,8,128]{4,3,2,1,0:T(8,128)S(1)}, u32[]{:S(2)}, u32[]{:S(2)}) collective-permute-start(f32[16,3,2,8,128]{4,3,2,1,0:T(8,128)} %coarse2.1), channel_id=1, source_target_pairs={{0,32},{16,48},{32,64},{48,80},{64,96},{80,112},{96,128},{112,144}... | collective-permute-start | bytes 1179656 | tf_op jit(solution)/shard_map/ppermute | solution.py:269
  183.2 9.7 %collective-permute-start.16 = (f32[16,3,2,8,128]{4,3,2,1,0:T(8,128)S(1)}, f32[16,3,2,8,128]{4,3,2,1,0:T(8,128)S(1)}, u32[]{:S(2)}, u32[]{:S(2)}) collective-permute-start(f32[16,3,2,8,128]{4,3,2,1,0:T(8,128)S(1)} %select_add_fusion.1.own), channel_id=1, source_target_pairs={{1,0},{2,1},{3,2},{4,3},{5,4},{6,5},{7,6},{8,7},{9,8},{10,9},{11,1... | collective-permute-start | bytes 1179656 | tf_op jit(solution)/shard_map/ppermute | solution.py:264
  184.5 9.8 %collective-permute-start.15 = (f32[16,3,2,8,128]{4,3,2,1,0:T(8,128)S(1)}, f32[16,3,2,8,128]{4,3,2,1,0:T(8,128)S(1)}, u32[]{:S(2)}, u32[]{:S(2)}) collective-permute-start(f32[16,3,2,8,128]{4,3,2,1,0:T(8,128)S(1)} %select_add_fusion.1.own), channel_id=1, source_target_pairs={{0,1},{1,2},{2,3},{3,4},{4,5},{5,6},{6,7},{7,8},{8,9},{9,10},{10,1... | collective-permute-start | bytes 1179656 | tf_op jit(solution)/shard_map/ppermute | solution.py:264
  217.8 56.2 %copy-start.2 = (f32[16,3,2,8,128]{4,3,2,1,0:T(8,128)S(1)}, f32[16,3,2,8,128]{4,3,2,1,0:T(8,128)}, u32[]{:S(2)}) copy-start(f32[16,3,2,8,128]{4,3,2,1,0:T(8,128)} %coarse4.3.own) | copy-start | bytes 1179652
  217.8 11.6 %collective-permute-start.19 = (f32[16,3,2,8,128]{4,3,2,1,0:T(8,128)}, f32[16,3,2,8,128]{4,3,2,1,0:T(8,128)S(1)}, u32[]{:S(2)}, u32[]{:S(2)}) collective-permute-start(f32[16,3,2,8,128]{4,3,2,1,0:T(8,128)} %coarse4.3.own), channel_id=1, source_target_pairs={{1,0},{2,1},{3,2},{4,3},{5,4},{6,5},{7,6},{8,7},{9,8},{10,9},{11,1... | collective-permute-start | bytes 1179656 | tf_op jit(solution)/shard_map/ppermute | solution.py:264
  219.2 11.8 %collective-permute-start.18 = (f32[16,3,2,8,128]{4,3,2,1,0:T(8,128)}, f32[16,3,2,8,128]{4,3,2,1,0:T(8,128)S(1)}, u32[]{:S(2)}, u32[]{:S(2)}) collective-permute-start(f32[16,3,2,8,128]{4,3,2,1,0:T(8,128)} %coarse4.3.own), channel_id=1, source_target_pairs={{0,1},{1,2},{2,3},{3,4},{4,5},{5,6},{6,7},{7,8},{8,9},{9,10},{10,1... | collective-permute-start | bytes 1179656 | tf_op jit(solution)/shard_map/ppermute | solution.py:264
  254.5 36.1 %collective-permute-start.22 = (f32[16,3,2,8,128]{4,3,2,1,0:T(8,128)}, f32[16,3,2,8,128]{4,3,2,1,0:T(8,128)S(1)}, u32[]{:S(2)}, u32[]{:S(2)}) collective-permute-start(f32[16,3,2,8,128]{4,3,2,1,0:T(8,128)} %coarse4.4.own), channel_id=1, source_target_pairs={{1,0},{2,1},{3,2},{4,3},{5,4},{6,5},{7,6},{8,7},{9,8},{10,9},{11,1... | collective-permute-start | bytes 1179656 | tf_op jit(solution)/shard_map/ppermute | solution.py:264
  255.8 34.8 %collective-permute-start.21 = (f32[16,3,2,8,128]{4,3,2,1,0:T(8,128)}, f32[16,3,2,8,128]{4,3,2,1,0:T(8,128)S(1)}, u32[]{:S(2)}, u32[]{:S(2)}) collective-permute-start(f32[16,3,2,8,128]{4,3,2,1,0:T(8,128)} %coarse4.4.own), channel_id=1, source_target_pairs={{0,1},{1,2},{2,3},{3,4},{4,5},{5,6},{6,7},{7,8},{8,9},{9,10},{10,1... | collective-permute-start | bytes 1179656 | tf_op jit(solution)/shard_map/ppermute | solution.py:264
  273.9 48.3 %collective-permute-start.14 = (f32[16,3,2,8,128]{4,3,2,1,0:T(8,128)S(1)}, f32[16,3,2,8,128]{4,3,2,1,0:T(8,128)S(1)}, u32[]{:S(2)}, u32[]{:S(2)}) collective-permute-start(f32[16,3,2,8,128]{4,3,2,1,0:T(8,128)S(1)} %copy-done.4), channel_id=1, source_target_pairs={{0,16},{16,32},{32,48},{48,64},{64,80},{80,96},{96,112},{112,128},... | collective-permute-start | bytes 1179656 | tf_op jit(solution)/shard_map/ppermute | solution.py:269
  274.0 48.2 %collective-permute-start.17 = (f32[16,3,2,8,128]{4,3,2,1,0:T(8,128)S(1)}, f32[16,3,2,8,128]{4,3,2,1,0:T(8,128)S(1)}, u32[]{:S(2)}, u32[]{:S(2)}) collective-permute-start(f32[16,3,2,8,128]{4,3,2,1,0:T(8,128)S(1)} %copy-done.2), channel_id=1, source_target_pairs={{0,80},{16,96},{32,112},{48,128},{64,144},{80,160},{96,176},{112,1... | collective-permute-start | bytes 1179656 | tf_op jit(solution)/shard_map/ppermute | solution.py:269
  284.7 37.6 %collective-permute-start.20 = (f32[16,3,2,8,128]{4,3,2,1,0:T(8,128)}, f32[16,3,2,8,128]{4,3,2,1,0:T(8,128)S(1)}, u32[]{:S(2)}, u32[]{:S(2)}) collective-permute-start(f32[16,3,2,8,128]{4,3,2,1,0:T(8,128)} %coarse4.4.own), channel_id=1, source_target_pairs={{0,144},{16,160},{32,176},{48,192},{64,208},{80,224},{96,240},{112... | collective-permute-start | bytes 1179656 | tf_op jit(solution)/shard_map/ppermute | solution.py:269
  314.8 12.6 %collective-permute-start.23 = (f32[16,3,2,8,128]{4,3,2,1,0:T(8,128)}, f32[16,3,2,8,128]{4,3,2,1,0:T(8,128)S(1)}, u32[]{:S(2)}, u32[]{:S(2)}) collective-permute-start(f32[16,3,2,8,128]{4,3,2,1,0:T(8,128)} %coarse4.5), channel_id=1, source_target_pairs={{0,208},{16,224},{32,240},{48,0},{64,16},{80,32},{96,48},{112,64},... | collective-permute-start | bytes 1179656 | tf_op jit(solution)/shard_map/ppermute | solution.py:269
  328.2 56.2 %all-to-all-start.3 = ((f32[16,3,2,8,128]{4,3,2,1,0:T(8,128)}), f32[16,3,2,8,128]{4,3,2,1,0:T(8,128)S(1)}, u32[]{:S(2)}, u32[]{:S(2)}) async-start(f32[16,3,2,8,128]{4,3,2,1,0:T(8,128)} %select_add_fusion.own), calls=%async_computation.3 | async-start | bytes 786432 | tf_op jit(solution)/shard_map/all_to_all | solution.py:273
  365.6 9.8 %collective-permute-start.25 = (f32[16,3,2,8,128]{4,3,2,1,0:T(8,128)}, f32[16,3,2,8,128]{4,3,2,1,0:T(8,128)S(1)}, u32[]{:S(2)}, u32[]{:S(2)}) collective-permute-start(f32[16,3,2,8,128]{4,3,2,1,0:T(8,128)} %select_add_fusion.own), channel_id=1, source_target_pairs={{1,0},{2,1},{3,2},{4,3},{5,4},{6,5},{7,6},{8,7},{9,8},{10,9},{11,1... | collective-permute-start | bytes 1179656 | tf_op jit(solution)/shard_map/ppermute | solution.py:264
  366.9 9.0 %collective-permute-start.24 = (f32[16,3,2,8,128]{4,3,2,1,0:T(8,128)}, f32[16,3,2,8,128]{4,3,2,1,0:T(8,128)S(1)}, u32[]{:S(2)}, u32[]{:S(2)}) collective-permute-start(f32[16,3,2,8,128]{4,3,2,1,0:T(8,128)} %select_add_fusion.own), channel_id=1, source_target_pairs={{0,1},{1,2},{2,3},{3,4},{4,5},{5,6},{6,7},{7,8},{8,9},{9,10},{10,1... | collective-permute-start | bytes 1179656 | tf_op jit(solution)/shard_map/ppermute | solution.py:264
  384.4 22.1 %all-to-all-start.4 = ((f32[16,3,2,8,128]{4,3,2,1,0:T(8,128)}), f32[16,3,2,8,128]{4,3,2,1,0:T(8,128)S(1)}, u32[]{:S(2)}, u32[]{:S(2)}) async-start(f32[16,3,2,8,128]{4,3,2,1,0:T(8,128)} %coarse1.3), calls=%async_computation.4 | async-start | bytes 786432 | tf_op jit(solution)/shard_map/all_to_all | solution.py:273
  (27 other events, 160.1 us)

commit v2 on v1

v2 whole, which is shorter than its diff:
```python
import functools

import jax
import jax.numpy as jnp
from jax import lax
from jax.experimental import pallas as pl
from jax.experimental.pallas import tpu as pltpu
from jax.sharding import PartitionSpec as P

FSTEPS = 2
FSWEEPS = 8
CSWEEPS = 2

floor_rate = 0.05
top_rate = 1.0
curl_bound = 14.0

ROWS = 8
UNROLL = 8


def chebyshev_weights(lower, upper, sweeps):
    theta, delta = 0.5 * (upper + lower), 0.5 * (upper - lower)
    sigma = theta / delta
    top = [1.0, sigma]
    for _ in range(sweeps):
        top.append(2.0 * sigma * top[-1] - top[-2])
    step = [1.0 / theta] + [0.0] * (sweeps - 1)
    weights = list(step)
    rho = 1.0 / sigma
    for k in range(1, sweeps):
        rho_next = 1.0 / (2.0 * sigma - rho)
        step = [rho_next * rho * v for v in step]
        step[k] += 2.0 * rho_next / delta / top[k]
        weights = [a + b for a, b in zip(weights, step)]
        rho = rho_next
    return theta, delta, weights, top[sweeps]


FINE = chebyshev_weights(FSTEPS * floor_rate, FSTEPS * top_rate + curl_bound, FSWEEPS)
COARSE = chebyshev_weights(floor_rate, top_rate + curl_bound, CSWEEPS)


def shifts(shape):
    rows, lanes = shape
    lane = lax.broadcasted_iota(jnp.int32, shape, 1)
    not_last, not_first = lane < lanes - 1, lane > 0

    def next_z(v):
        return jnp.where(not_last, pltpu.roll(v, lanes - 1, axis=1), 0.0)

    def prev_z(v):
        return jnp.where(not_first, pltpu.roll(v, 1, axis=1), 0.0)

    def next_y(v):
        return pltpu.roll(v, rows - 1, axis=0)

    def prev_y(v):
        return pltpu.roll(v, 1, axis=0)

    return next_z, prev_z, next_y, prev_y


def window(margin):
    if margin >= ROWS // 2:
        return 0, 3 * ROWS
    if margin > 0:
        return ROWS // 2, 2 * ROWS
    return 0, 2 * ROWS


def curl_sweep(field, rel, keep_top, margin, emit, planes):
    low, count = window(margin)
    high = low + count
    next_z, prev_z, _, prev_y = shifts((count, 128))
    tail = lax.broadcasted_iota(jnp.int32, (ROWS, 128), 0) + (high - ROWS)
    tail = jnp.where(tail < 2 * ROWS, 1.0, keep_top)
    rows = pl.ds(low, count) if margin else pl.ds(ROWS, ROWS)

    def prev_y_in(v):
        w = prev_y(v)
        if margin:
            w = jnp.concatenate((w[: count - ROWS], w[count - ROWS :] * tail), 0)
        return w

    def crop(v):
        return v if margin else v[ROWS:]

    def body(m, carry):
        hy_low, hz_low = carry
        for j in range(UNROLL):
            i = m * UNROLL + j
            ex, ey, ez = [field[i, comp, low:high] for comp in range(3)]
            ey_up, ez_up = [field[i + 1, comp, low:high] for comp in (1, 2)]
            ex_next, ez_next = [field[i, comp, low + 1 : high + 1] for comp in (0, 2)]
            nu = rel[i, low:high]
            hx = nu * ((ez_next - ez) - (next_z(ey) - ey))
            hy = nu * ((next_z(ex) - ex) - (ez_up - ez))
            hz = nu * ((ey_up - ey) - (ex_next - ex))
            kx = crop(prev_z(hy) - hy) - crop(prev_y_in(hz) - hz)
            ky = crop(hz_low - hz) - crop(prev_z(hx) - hx)
            kz = crop(prev_y_in(hx) - hx) - crop(hy_low - hy)
            emit(i, rows, (kx, ky, kz))
            hy_low, hz_low = hy, hz
        return hy_low, hz_low

    zero = jnp.zeros((count, 128), jnp.float32)
    lax.fori_loop(0, planes // UNROLL, body, (zero, zero))


def load_rows(dst, other, low, own, high, blocks):
    zero = jnp.zeros((ROWS, 128), jnp.float32)
    edge = low.shape[3]

    def body(b, _):
        for j in range(2):
            for comp in range(3):
                i = 2 * b + j
                if edge < ROWS:
                    dst[i, comp, 0:ROWS] = zero
                    dst[i, comp, 2 * ROWS : 3 * ROWS] = zero
                dst[i, comp, ROWS - edge : ROWS] = low[b, comp, j]
                dst[i, comp, ROWS : 2 * ROWS] = own[b, comp, j]
                dst[i, comp, 2 * ROWS : 2 * ROWS + edge] = high[b, comp, j]
                dst[i, comp, 3 * ROWS : 4 * ROWS] = zero
                other[i, comp, 3 * ROWS : 4 * ROWS] = zero
        return 0

    lax.fori_loop(0, blocks, body, 0)
    for comp in range(3):
        dst[2 * blocks, comp] = jnp.zeros((4 * ROWS, 128), jnp.float32)
        other[2 * blocks, comp] = jnp.zeros((4 * ROWS, 128), jnp.float32)


MID = pl.ds(ROWS, ROWS)


def fine_kernel(first, flags, low, own, high, con, rel, *rest):
    if first:
        total, after, here, there, quot, nu2 = rest
    else:
        other, base, out, total, here, there, quot, nu2 = rest
    blocks = own.shape[0]
    planes = 2 * blocks
    theta, delta, weights, scale = FINE
    load_rows(here, there, low, own, high, blocks)

    def prepare(i, _):
        quot[i] = 2.0 * theta / delta - (2.0 * FSTEPS / delta) * con[i]
        nu2[i] = (2.0 / delta) * rel[i]
        return 0

    lax.fori_loop(0, planes, prepare, 0)

    buffers = (here, there)
    sweeps = FSWEEPS if first else FSWEEPS - 1
    for k in range(sweeps):
        now, new = buffers[k % 2], buffers[(k + 1) % 2]

        def emit(i, rows, curl, k=k, now=now, new=new):
            b, j = i // 2, i % 2
            q = quot[i, rows]
            for comp in range(3):
                v = q * now[i, comp, rows] - curl[comp]
                v = 0.5 * v if k == 0 else v - new[i, comp, rows]
                acc = weights[k] * now[i, comp, MID]
                if k > 0:
                    acc = total[b, comp, j] + acc
                elif not first:
                    acc = other[b, comp, j] + acc
                if k + 1 < sweeps:
                    new[i, comp, rows] = v
                elif first:
                    after[b, comp, j] = (1.0 / scale) * v + (FSTEPS * con[i, MID]) * acc
                else:
                    acc = acc + weights[k + 1] * v
                    out[b, comp, j] = base[b, comp, j] + acc
                total[b, comp, j] = acc

        curl_sweep(now, nu2, flags[0], sweeps - 1 - k, emit, planes)


def coarse_kernel(count, gate, flags, low, own, high, con, rel, *rest):
    if gate is None:
        out, state, curled, fac, nu3 = rest
    else:
        extra, out, state, curled, fac, nu3 = rest
    blocks = own.shape[0]
    planes = 2 * blocks
    theta, delta, weights, _ = COARSE
    load_rows(state, curled, low, own, high, blocks)

    def prepare(i, _):
        fac[i] = (weights[0] + weights[1] * theta / delta) - (weights[1] / delta) * con[i]
        nu3[i] = (weights[1] / delta) * rel[i]
        return 0

    lax.fori_loop(0, planes, prepare, 0)

    for n in range(count):
        margin = 2 * (count - 1 - n)

        def first(i, rows, curl):
            for comp in range(3):
                curled[i, comp, rows] = curl[comp]

        curl_sweep(state, rel, flags[0], margin + 1, first, planes)

        def second(i, rows, curl, margin=margin):
            f = fac[i, rows]
            for comp in range(3):
                v = state[i, comp, rows] - f * curled[i, comp, rows] + curl[comp]
                if margin:
                    state[i, comp, rows] = v
                elif gate is None:
                    out[i // 2, comp, i % 2] = v
                else:
                    out[i // 2, comp, i % 2] = extra[i // 2, comp, i % 2] + jnp.where(flags[gate] > 0.0, v, 0.0)

        curl_sweep(curled, nu3, flags[0], margin, second, planes)


def plane_curls(ny):
    next_z, prev_z, raw_next, raw_prev = shifts((ny, 128))
    row = lax.broadcasted_iota(jnp.int32, (ny, 128), 0)

    def next_y(v):
        return jnp.where(row < ny - 1, raw_next(v), 0.0)

    def prev_y(v):
        return jnp.where(row > 0, raw_prev(v), 0.0)

    def curl(nu, e, up):
        ex, ey, ez = e
        hx = nu * ((next_y(ez) - ez) - (next_z(ey) - ey))
        hy = nu * ((next_z(ex) - ex) - (up[1] - ez))
        hz = nu * ((up[0] - ey) - (next_y(ex) - ex))
        return hx, hy, hz

    def back(h, low):
        hx, hy, hz = h
        kx = (prev_z(hy) - hy) - (prev_y(hz) - hz)
        ky = (low[2] - hz) - (prev_z(hx) - hx)
        kz = (prev_y(hx) - hx) - (low[1] - hy)
        return kx, ky, kz

    return curl, back


def spread(ref, comp, i, v):
    for b in range(v.shape[0] // ROWS):
        ref[b, comp, i] = v[b * ROWS : (b + 1) * ROWS]


def residual_kernel(flags, state, src, rel, up, low, rel_low, res):
    planes, ny = rel.shape[0], rel.shape[1]
    curl, back = plane_curls(ny)
    before = curl(rel_low[0], (low[0], low[1], low[2]), (state[1, 0], state[2, 0]))
    for i in range(planes):
        nxt = (state[1, i + 1], state[2, i + 1]) if i + 1 < planes else (up[0], up[1])
        here = curl(rel[i], (state[0, i], state[1, i], state[2, i]), nxt)
        k = back(here, before)
        for comp in range(3):
            spread(res, comp, i, src[comp, i] - k[comp])
        before = here


def base_kernel(flags, state, old, src, con, rel, up, low, rel_low, begin, begin_up, begin_low, base, work):
    planes, ny = con.shape[0], con.shape[1]
    theta, delta, weights, _ = COARSE
    curl, back = plane_curls(ny)

    def fac(i):
        return (weights[0] + weights[1] * theta / delta) - (weights[1] / delta) * con[i]

    before = curl(rel_low[0], (low[0], low[1], low[2]), (src[1, 0], src[2, 0]))
    for i in range(planes):
        nxt = (src[1, i + 1], src[2, i + 1]) if i + 1 < planes else (up[0], up[1])
        here = curl(rel[i], (src[0, i], src[1, i], src[2, i]), nxt)
        k = back(here, before)
        for comp in range(3):
            push = fac(i) * src[comp, i] - (weights[1] / delta) * k[comp]
            spread(base, comp, i, state[comp, i] - old[comp, i] + push)
        before = here

    @pl.when(flags[1] > 0.0)
    def _():
        def part(i, comp):
            if i < 0:
                return begin_low[comp * planes + planes + i]
            return begin[comp, i] if i < planes else begin_up[comp * planes + i - planes]

        def nu(i):
            if i < 0:
                return begin_low[3 * planes + planes + i]
            return rel[i] if i < planes else begin_up[3 * planes + i - planes]

        def h_of(i):
            above = (part(i + 1, 1), part(i + 1, 2))
            return curl(nu(i), (part(i, 0), part(i, 1), part(i, 2)), above)

        before = h_of(-2)
        for i in range(-1, planes + 1):
            here = h_of(i)
            k = back(here, before)
            for comp in range(3):
                work[i + 1, comp] = k[comp] * flags[2] if i == planes else k[comp]
            before = here
        before = None
        for i in range(-1, planes):
            u = [work[i + 1, comp] for comp in range(3)]
            here = curl(nu(i), u, (work[i + 2, 1], work[i + 2, 2]))
            if i >= 0:
                k = back(here, before)
                for comp in range(3):
                    v = begin[comp, i] - fac(i) * u[comp] + (weights[1] / delta) * k[comp]
                    for b in range(ny // ROWS):
                        base[b, comp, i] = base[b, comp, i] + v[b * ROWS : (b + 1) * ROWS]
            before = here


VMEM = pl.BlockSpec(memory_space=pltpu.VMEM)
SMEM = pl.BlockSpec(memory_space=pltpu.SMEM)


def call(kernel, name, outs, scratch, flags, *operands):
    return pl.pallas_call(
        kernel,
        name=name,
        out_shape=[jax.ShapeDtypeStruct(s, jnp.float32) for s in outs],
        in_specs=[SMEM] + [VMEM] * len(operands),
        out_specs=[VMEM] * len(outs),
        scratch_shapes=[pltpu.VMEM(s, jnp.float32) for s in scratch],
    )(flags, *operands)


def open_shift(value, steps):
    count = lax.axis_size("space")
    first, last = max(0, -steps), min(count, count - steps)
    return lax.ppermute(value, "space", [(i, i + steps) for i in range(first, last)])


def ring_shift(value, steps):
    count = lax.axis_size("slab")
    return lax.ppermute(value, "slab", [(i, (i + steps) % count) for i in range(count)])


def both_shift(value, steps, along):
    slabs, spaces = lax.axis_size("slab"), lax.axis_size("space")
    pairs = [
        (i * spaces + k, (i + steps) % slabs * spaces + k + along)
        for i in range(slabs)
        for k in range(spaces)
        if 0 <= k + along < spaces
    ]
    return lax.ppermute(value, ("slab", "space"), pairs)


def turn(value):
    return lax.all_to_all(value, "space", 0, 0, tiled=True)


def halo(value):
    return open_shift(value, 1), open_shift(value, -1)


def local(state_old, coarse_old, source, start_state, conduct, reluct, converged):
    groups = lax.axis_size("slab")
    spaces = lax.axis_size("space")
    position = (lax.axis_index("slab") - converged[0] % groups - 1) % groups
    inner = lax.axis_index("space") < spaces - 1
    flags = jnp.stack((inner, position == 0, inner, position >= 1, position >= 2)).astype(jnp.float32)
    state, old, src = state_old[0], coarse_old[0], source[0]
    planes, ny = conduct.shape[0], conduct.shape[1]
    blocks = spaces
    nx = blocks * planes
    field = (blocks, 3, planes, ROWS, 128)

    ups = open_shift(jnp.stack((state[1:3, 0], src[1:3, 0])), -1)
    lows = open_shift(jnp.concatenate((state[:, -1], src[:, -1], reluct[-1:])), 1)
    coef = jnp.stack((conduct, reluct)).reshape(2, planes, blocks, ROWS, 128).transpose(2, 0, 1, 3, 4)
    coef = turn(coef)
    coef_low, coef_high = halo(coef)
    coef24 = jnp.concatenate((coef_low, coef, coef_high), 3).transpose(1, 0, 2, 3, 4).reshape(2, nx, 3 * ROWS, 128)
    con, rel = coef24[0], coef24[1]

    (res,) = call(residual_kernel, "residual", [field], [], flags, state, src, reluct, ups[0], lows[0:3], lows[6:7])
    res = turn(res)
    res_low, res_high = halo(res)

    start_state, res = lax.optimization_barrier((start_state, res))
    edge = jnp.concatenate((start_state.reshape(3 * planes, ny, 128), reluct))
    edge_low, edge_high = halo(edge)

    wide = (nx + 1, 3, 4 * ROWS, 128)
    slim = (nx, 3 * ROWS, 128)
    scratch = [wide, wide, slim, slim]
    total, after = call(
        functools.partial(fine_kernel, True), "fine_first", [field, field], scratch, flags,
        res_low, res, res_high, con, rel,
    )
    after_low, after_high = halo(after)
    src, after = lax.optimization_barrier((src, after))
    (base,) = call(
        base_kernel, "base", [field], [(planes + 2, 3, ny, 128)], flags,
        state, old, src, conduct, reluct, ups[1], lows[3:6], lows[6:7], start_state, edge_high, edge_low,
    )
    base = turn(base)

    lead, total = call(
        functools.partial(fine_kernel, False), "fine_second", [field, field], scratch, flags,
        after_low, after, after_high, con, rel, total, base,
    )

    def coarse(value, count):
        low, high = halo(value)
        return call(
            functools.partial(coarse_kernel, count, None), "coarse%d" % count, [field], scratch, flags,
            low, value, high, con, rel,
        )[0]

    def joined(value, steps, gate):
        rows = 2 * steps
        own = ring_shift(value, steps)
        low = both_shift(value[:, :, :, ROWS - rows :], steps, 1)
        high = both_shift(value[:, :, :, :rows], steps, -1)
        return call(
            functools.partial(coarse_kernel, steps, gate), "joined%d" % steps, [field], scratch, flags,
            low, own, high, con, rel, value,
        )[0]

    lead = joined(lead, 1, 3)
    lead = joined(lead, 2, 4)
    final, power = lead, lead
    for steps in range(4, groups, 4):
        power = coarse(power, 4)
        final = final + jnp.where(position >= steps, ring_shift(power, steps), 0.0)
    starts = ring_shift(final, 1)
    ends = final - total

    def home(value):
        return turn(value).transpose(1, 2, 0, 3, 4).reshape(3, planes, ny, 128)

    coarse_new = home(ends) + (old - state)
    state_new = jnp.where(position == 0, start_state, home(starts))
    return state_new[None], coarse_new[None]


def solution(mesh):
    placed = (
        P("slab", None, "space", None, None),
        P("slab", None, "space", None, None),
        P("slab", None, "space", None, None),
        P(None, "space", None, None),
        P("space", None, None),
        P("space", None, None),
        P(),
    )
    return jax.shard_map(
        local,
        mesh=mesh,
        in_specs=placed,
        out_specs=(P("slab", None, "space", None, None), P("slab", None, "space", None, None)),
        check_vma=False,
    )
```

time: 409 us -> 332 us (0.81)
  the two profiles are of different devices: /device:TPU:1 before, /device:TPU:160 now
where the time goes in v2:
time: 332 us; the launch traced here: 329 us
  waiting for transfers between devices  142 us (43%)
  starting transfers between devices  105 us (32%)
  Pallas kernels  58.1 us (18%)
  local copies, waits for them, and re-layouts  17.2 us (5%)
  other arithmetic  4.24 us (1%)
    ppermute x16, starting transfers between devices, open_shift(): lax.ppermute(value, 'space', [(i, i + steps) for i in range(first, last)])  62.1 us
    pallas_call x9, Pallas kernels, call(): pl.pallas_call(kernel, name=name, out_shape=[jax.ShapeDtypeStruct(s, jnp....  58.1 us
    ppermute x16, waiting for transfers between devices, open_shift(): lax.ppermute(value, 'space', [(i, i + steps) for i in range(first, last)])  55.8 us
    ppermute x4, waiting for transfers between devices, both_shift(): return lax.ppermute(value, ('slab', 'space'), pairs)  45.5 us
    ppermute x6, waiting for transfers between devices, ring_shift(): lax.ppermute(value, 'slab', [(i, (i + steps) % count) for i in range(coun...  31.2 us
    all_to_all x5, starting transfers between devices, turn(): return lax.all_to_all(value, 'space', 0, 0, tiled=True)  29.2 us
    ppermute x4, starting transfers between devices, both_shift(): return lax.ppermute(value, ('slab', 'space'), pairs)  12.4 us
    all_to_all x5, waiting for transfers between devices, turn(): return lax.all_to_all(value, 'space', 0, 0, tiled=True)  9.52 us
  transfers between devices with their start and end apart: 31, of which 17 were waited for; matrix products, arithmetic and copies ran while one was open for 3% of the time, Pallas kernels for 6%

profile of v2, /device:TPU:160, one launch (start us, length us, event | category | flops | bytes accessed | tf_op | source)
XLA Modules:
  0.0 328.6 jit_solution(1195724501133949649)
XLA Ops:
  1.8 5.4 %collective-permute-start = (f32[2,2,128,128]{3,2,1,0:T(8,128)S(1)}, f32[2,2,128,128]{3,2,1,0:T(8,128)S(1)}, u32[]{:S(2)}, u32[]{:S(2)}) collective-permute-start(f32[2,2,128,128]{3,2,1,0:T(8,128)S(1)} %pad_maximum_fusion.2), channel_id=1, source_target_pairs={{1,0},{2,1},{3,2},{4,3},{5,4},{6,5},{7,6},{8,7},{9,8},{10,9},{11,1... | collective-permute-start | bytes 786440 | tf_op jit(solution)/shard_map/ppermute | solution.py:340
  11.0 6.9 %all-to-all-start.1 = ((f32[16,2,2,8,128]{4,3,2,1,0:T(8,128)}), f32[16,2,2,8,128]{4,3,2,1,0:T(8,128)S(1)}, u32[]{:S(2)}, u32[]{:S(2)}) async-start(f32[16,2,2,8,128]{4,3,2,1,0:T(8,128)} %copy.39), calls=%async_computation.1 | async-start | bytes 524288 | tf_op jit(solution)/shard_map/all_to_all | solution.py:360
  20.0 6.5 %collective-permute-done.1 = f32[7,128,128]{2,1,0:T(8,128)S(1)} collective-permute-done((f32[7,128,128]{2,1,0:T(8,128)S(1)}, f32[7,128,128]{2,1,0:T(8,128)S(1)}, u32[]{:S(2)}, u32[]{:S(2)}) %collective-permute-start.1) | collective-permute-done | bytes 458784 | tf_op jit(solution)/shard_map/ppermute | solution.py:340
  30.2 5.6 %all-to-all-start = ((f32[16,3,2,8,128]{4,3,2,1,0:T(8,128)}), f32[16,3,2,8,128]{4,3,2,1,0:T(8,128)S(1)}, u32[]{:S(2)}, u32[]{:S(2)}) async-start(f32[16,3,2,8,128]{4,3,2,1,0:T(8,128)} %residual.1), calls=%async_computation | async-start | bytes 786432 | tf_op jit(solution)/shard_map/all_to_all | solution.py:360
  39.2 4.6 %collective-permute-start.5 = (f32[16,2,2,8,128]{4,3,2,1,0:T(8,128)S(1)}, f32[16,2,2,8,128]{4,3,2,1,0:T(8,128)}, u32[]{:S(2)}, u32[]{:S(2)}) collective-permute-start(f32[16,2,2,8,128]{4,3,2,1,0:T(8,128)S(1)} %all-to-all-done.1), channel_id=1, source_target_pairs={{1,0},{2,1},{3,2},{4,3},{5,4},{6,5},{7,6},{8,7},{9,8},{10,9},{11,1... | collective-permute-start | bytes 786440 | tf_op jit(solution)/shard_map/ppermute | solution.py:340
  54.2 4.8 %collective-permute-start.3 = (f32[16,3,2,8,128]{4,3,2,1,0:T(8,128)S(1)}, f32[16,3,2,8,128]{4,3,2,1,0:T(8,128)S(1)}, u32[]{:S(2)}, u32[]{:S(2)}) collective-permute-start(f32[16,3,2,8,128]{4,3,2,1,0:T(8,128)S(1)} %all-to-all-done.own), channel_id=1, source_target_pairs={{1,0},{2,1},{3,2},{4,3},{5,4},{6,5},{7,6},{8,7},{9,8},{10,9},{11,1... | collective-permute-start | bytes 1179656 | tf_op jit(solution)/shard_map/ppermute | solution.py:340
  61.1 9.1 %collective-permute-done.2.low = f32[16,3,2,8,128]{4,3,2,1,0:T(8,128)S(1)} collective-permute-done((f32[16,3,2,8,128]{4,3,2,1,0:T(8,128)S(1)}, f32[16,3,2,8,128]{4,3,2,1,0:T(8,128)S(1)}, u32[]{:S(2)}, u32[]{:S(2)}) %collective-permute-start.2) | collective-permute-done | bytes 393248 | tf_op jit(solution)/shard_map/ppermute | solution.py:340
  71.0 8.9 %fine_first.1 = (f32[16,3,2,8,128]{4,3,2,1,0:T(8,128)}, f32[16,3,2,8,128]{4,3,2,1,0:T(8,128)}) custom-call(f32[5]{0:T(128)} %convert_element_type.3.flags, f32[16,3,2,8,128]{4,3,2,1,0:T(8,128)} %copy-done.22, f32[16,3,2,8,128]{4,3,2,1,0:T(8,128)} %copy-done.8, f32[16,3,2,8,128]{4,3,2,1,0:T(8,128)} %copy-done.23, f32[32,24,128]{2,1,0:T(8,128)} %bitcast.59, ...), custom_call_target="tpu_custom_call" | custom-call | tf_op jit(solution)/shard_map/fine_first/pallas_call | solution.py:327
  84.7 4.5 %all-to-all-start.2 = ((f32[16,3,2,8,128]{4,3,2,1,0:T(8,128)}), f32[16,3,2,8,128]{4,3,2,1,0:T(8,128)S(1)}, u32[]{:S(2)}, u32[]{:S(2)}) async-start(f32[16,3,2,8,128]{4,3,2,1,0:T(8,128)} %base.1), calls=%async_computation.2 | async-start | bytes 786432 | tf_op jit(solution)/shard_map/all_to_all | solution.py:360
  92.6 4.6 %collective-permute-start.7 = (f32[16,3,2,8,128]{4,3,2,1,0:T(8,128)S(1)}, f32[16,3,2,8,128]{4,3,2,1,0:T(8,128)S(1)}, u32[]{:S(2)}, u32[]{:S(2)}) collective-permute-start(f32[16,3,2,8,128]{4,3,2,1,0:T(8,128)S(1)} %copy-done.25), channel_id=1, source_target_pairs={{1,0},{2,1},{3,2},{4,3},{5,4},{6,5},{7,6},{8,7},{9,8},{10,9},{11,1... | collective-permute-start | bytes 1179656 | tf_op jit(solution)/shard_map/ppermute | solution.py:340
  97.2 6.7 %collective-permute-done.6.low = f32[16,3,2,8,128]{4,3,2,1,0:T(8,128)S(1)} collective-permute-done((f32[16,3,2,8,128]{4,3,2,1,0:T(8,128)S(1)}, f32[16,3,2,8,128]{4,3,2,1,0:T(8,128)S(1)}, u32[]{:S(2)}, u32[]{:S(2)}) %collective-permute-start.6) | collective-permute-done | bytes 393248 | tf_op jit(solution)/shard_map/ppermute | solution.py:340
  104.8 8.6 %fine_second.1 = (f32[16,3,2,8,128]{4,3,2,1,0:T(8,128)}, f32[16,3,2,8,128]{4,3,2,1,0:T(8,128)}) custom-call(f32[5]{0:T(128)} %convert_element_type.3.flags, f32[16,3,2,8,128]{4,3,2,1,0:T(8,128)} %copy-done.26, f32[16,3,2,8,128]{4,3,2,1,0:T(8,128)} %get-tuple-element.13.own, f32[16,3,2,8,128]{4,3,2,1,0:T(8,128)} %copy-done.27, f32[32,24,128]{2,1,0:T(8,128)} %bitcast.60, ...), custom_call_target="tpu_custom_call" | custom-call | tf_op jit(solution)/shard_map/fine_second/pallas_call | solution.py:327
  118.3 5.0 %collective-permute-start.12 = (f32[16,3,2,2,128]{4,3,2,1,0:T(2,128)S(1)}, f32[16,3,2,2,128]{4,3,2,1,0:T(2,128)S(1)}, u32[]{:S(2)}, u32[]{:S(2)}) collective-permute-start(f32[16,3,2,2,128]{4,3,2,1,0:T(2,128)S(1)} %get-tuple-element.26), channel_id=1, source_target_pairs={{1,16},{2,17},{3,18},{4,19},{5,20},{6,21},{7,22},{8,23},{9,24},{10... | collective-permute-start | bytes 294920 | tf_op jit(solution)/shard_map/ppermute | solution.py:356
  123.3 14.2 %collective-permute-done.10.low = f32[16,3,2,2,128]{4,3,2,1,0:T(2,128)S(1)} collective-permute-done((f32[16,3,2,2,128]{4,3,2,1,0:T(2,128)S(1)}, f32[16,3,2,2,128]{4,3,2,1,0:T(2,128)S(1)}, u32[]{:S(2)}, u32[]{:S(2)}) %collective-permute-start.10) | collective-permute-done | bytes 98336 | tf_op jit(solution)/shard_map/ppermute | solution.py:356
  138.9 4.0 %joined1.1.rest_0_ = f32[16,3,2,8,128]{4,3,2,1,0:T(8,128)} custom-call(f32[5]{0:T(128)} %convert_element_type.3.flags, f32[16,3,2,2,128]{4,3,2,1,0:T(2,128)} %copy-done.30, f32[16,3,2,8,128]{4,3,2,1,0:T(8,128)} %copy-done.14, f32[16,3,2,2,128]{4,3,2,1,0:T(2,128)} %copy-done.31, f32[32,24,128]{2,1,0:T(8,128)} %bitcast.61, f32[32,24,128]{2,1,0:T(8,128)} %bitcast.54, ...), custom_call_target="tpu_custom_call" | custom-call | tf_op jit(solution)/shard_map/joined1/pallas_call | solution.py:327
  147.9 31.4 %collective-permute-done.13.low = f32[16,3,2,4,128]{4,3,2,1,0:T(4,128)S(1)} collective-permute-done((f32[16,3,2,4,128]{4,3,2,1,0:T(4,128)S(1)}, f32[16,3,2,4,128]{4,3,2,1,0:T(4,128)S(1)}, u32[]{:S(2)}, u32[]{:S(2)}) %collective-permute-start.13) | collective-permute-done | bytes 196640 | tf_op jit(solution)/shard_map/ppermute | solution.py:356
  180.8 5.5 %joined2.1.own = f32[16,3,2,8,128]{4,3,2,1,0:T(8,128)} custom-call(f32[5]{0:T(128)} %convert_element_type.3.flags, f32[16,3,2,4,128]{4,3,2,1,0:T(4,128)} %copy-done.28, f32[16,3,2,8,128]{4,3,2,1,0:T(8,128)} %copy-done.15, f32[16,3,2,4,128]{4,3,2,1,0:T(4,128)} %copy-done.29, f32[32,24,128]{2,1,0:T(8,128)} %bitcast.62, f32[32,24,128]{2,1,0:T(8,128)} %bitcast.55, ...), custom_call_target="tpu_custom_call" | custom-call | tf_op jit(solution)/shard_map/joined2/pallas_call | solution.py:327
  188.2 6.0 %collective-permute-start.17 = (f32[16,3,2,8,128]{4,3,2,1,0:T(8,128)}, f32[16,3,2,8,128]{4,3,2,1,0:T(8,128)S(1)}, u32[]{:S(2)}, u32[]{:S(2)}) collective-permute-start(f32[16,3,2,8,128]{4,3,2,1,0:T(8,128)} %joined2.1.own), channel_id=1, source_target_pairs={{1,0},{2,1},{3,2},{4,3},{5,4},{6,5},{7,6},{8,7},{9,8},{10,9},{11,1... | collective-permute-start | bytes 1179656 | tf_op jit(solution)/shard_map/ppermute | solution.py:340
  194.2 7.3 %collective-permute-done.16.low = f32[16,3,2,8,128]{4,3,2,1,0:T(8,128)S(1)} collective-permute-done((f32[16,3,2,8,128]{4,3,2,1,0:T(8,128)}, f32[16,3,2,8,128]{4,3,2,1,0:T(8,128)S(1)}, u32[]{:S(2)}, u32[]{:S(2)}) %collective-permute-start.16) | collective-permute-done | bytes 393248 | tf_op jit(solution)/shard_map/ppermute | solution.py:340
  203.6 8.6 %coarse4.3.own = f32[16,3,2,8,128]{4,3,2,1,0:T(8,128)} custom-call(f32[5]{0:T(128)} %convert_element_type.3.flags, f32[16,3,2,8,128]{4,3,2,1,0:T(8,128)} %copy-done.18, f32[16,3,2,8,128]{4,3,2,1,0:T(8,128)} %joined2.1.own, f32[16,3,2,8,128]{4,3,2,1,0:T(8,128)} %copy-done.20, f32[32,24,128]{2,1,0:T(8,128)} %bitcast.63, f32[32,24,128]{2,1,0:T(8,128)} %bitcast.56), custom_call_target="tpu_custom_call" | custom-call | tf_op jit(solution)/shard_map/coarse4/pallas_call | solution.py:327
  214.2 6.6 %collective-permute-start.20 = (f32[16,3,2,8,128]{4,3,2,1,0:T(8,128)}, f32[16,3,2,8,128]{4,3,2,1,0:T(8,128)S(1)}, u32[]{:S(2)}, u32[]{:S(2)}) collective-permute-start(f32[16,3,2,8,128]{4,3,2,1,0:T(8,128)} %coarse4.3.own), channel_id=1, source_target_pairs={{1,0},{2,1},{3,2},{4,3},{5,4},{6,5},{7,6},{8,7},{9,8},{10,9},{11,1... | collective-permute-start | bytes 1179656 | tf_op jit(solution)/shard_map/ppermute | solution.py:340
  220.8 6.2 %collective-permute-done.19.low = f32[16,3,2,8,128]{4,3,2,1,0:T(8,128)S(1)} collective-permute-done((f32[16,3,2,8,128]{4,3,2,1,0:T(8,128)}, f32[16,3,2,8,128]{4,3,2,1,0:T(8,128)S(1)}, u32[]{:S(2)}, u32[]{:S(2)}) %collective-permute-start.19) | collective-permute-done | bytes 393248 | tf_op jit(solution)/shard_map/ppermute | solution.py:340
  229.0 8.6 %coarse4.4.own = f32[16,3,2,8,128]{4,3,2,1,0:T(8,128)} custom-call(f32[5]{0:T(128)} %convert_element_type.3.flags, f32[16,3,2,8,128]{4,3,2,1,0:T(8,128)} %copy-done.19, f32[16,3,2,8,128]{4,3,2,1,0:T(8,128)} %coarse4.3.own, f32[16,3,2,8,128]{4,3,2,1,0:T(8,128)} %copy-done.21, f32[32,24,128]{2,1,0:T(8,128)} %bitcast.64, f32[32,24,128]{2,1,0:T(8,128)} %bitcast.57), custom_call_target="tpu_custom_call" | custom-call | tf_op jit(solution)/shard_map/coarse4/pallas_call | solution.py:327
  239.7 6.4 %collective-permute-start.23 = (f32[16,3,2,8,128]{4,3,2,1,0:T(8,128)}, f32[16,3,2,8,128]{4,3,2,1,0:T(8,128)S(1)}, u32[]{:S(2)}, u32[]{:S(2)}) collective-permute-start(f32[16,3,2,8,128]{4,3,2,1,0:T(8,128)} %coarse4.4.own), channel_id=1, source_target_pairs={{1,0},{2,1},{3,2},{4,3},{5,4},{6,5},{7,6},{8,7},{9,8},{10,9},{11,1... | collective-permute-start | bytes 1179656 | tf_op jit(solution)/shard_map/ppermute | solution.py:340
  247.5 15.2 %collective-permute-done.22.low = f32[16,3,2,8,128]{4,3,2,1,0:T(8,128)S(1)} collective-permute-done((f32[16,3,2,8,128]{4,3,2,1,0:T(8,128)}, f32[16,3,2,8,128]{4,3,2,1,0:T(8,128)S(1)}, u32[]{:S(2)}, u32[]{:S(2)}) %collective-permute-start.22) | collective-permute-done | bytes 393248 | tf_op jit(solution)/shard_map/ppermute | solution.py:340
  265.8 8.6 %coarse4.5 = f32[16,3,2,8,128]{4,3,2,1,0:T(8,128)} custom-call(f32[5]{0:T(128)} %convert_element_type.3.flags, f32[16,3,2,8,128]{4,3,2,1,0:T(8,128)} %copy-done.16, f32[16,3,2,8,128]{4,3,2,1,0:T(8,128)} %coarse4.4.own, f32[16,3,2,8,128]{4,3,2,1,0:T(8,128)} %copy-done.17, f32[32,24,128]{2,1,0:T(8,128)} %bitcast.65, f32[32,24,128]{2,1,0:T(8,128)} %bitcast.58), custom_call_target="tpu_custom_call" | custom-call | tf_op jit(solution)/shard_map/coarse4/pallas_call | solution.py:327
  277.9 3.9 %collective-permute-done.21 = f32[16,3,2,8,128]{4,3,2,1,0:T(8,128)S(1)} collective-permute-done((f32[16,3,2,8,128]{4,3,2,1,0:T(8,128)}, f32[16,3,2,8,128]{4,3,2,1,0:T(8,128)S(1)}, u32[]{:S(2)}, u32[]{:S(2)}) %collective-permute-start.21) | collective-permute-done | bytes 393248 | tf_op jit(solution)/shard_map/ppermute | solution.py:345
  281.8 4.9 %collective-permute-done.24 = f32[16,3,2,8,128]{4,3,2,1,0:T(8,128)S(1)} collective-permute-done((f32[16,3,2,8,128]{4,3,2,1,0:T(8,128)}, f32[16,3,2,8,128]{4,3,2,1,0:T(8,128)S(1)}, u32[]{:S(2)}, u32[]{:S(2)}) %collective-permute-start.24) | collective-permute-done | bytes 393248 | tf_op jit(solution)/shard_map/ppermute | solution.py:345
  287.6 3.8 %all-to-all-start.4 = ((f32[16,3,2,8,128]{4,3,2,1,0:T(8,128)}), f32[16,3,2,8,128]{4,3,2,1,0:T(8,128)S(1)}, u32[]{:S(2)}, u32[]{:S(2)}) async-start(f32[16,3,2,8,128]{4,3,2,1,0:T(8,128)} %get-tuple-element.18), calls=%async_computation.4 | async-start | bytes 786432 | tf_op jit(solution)/shard_map/all_to_all | solution.py:360
  291.5 18.9 %collective-permute-done.25 = f32[16,3,2,8,128]{4,3,2,1,0:T(8,128)} collective-permute-done((f32[16,3,2,8,128]{4,3,2,1,0:T(8,128)S(1)}, f32[16,3,2,8,128]{4,3,2,1,0:T(8,128)}, u32[]{:S(2)}, u32[]{:S(2)}) %collective-permute-start.25) | collective-permute-done | bytes 393248 | tf_op jit(solution)/shard_map/ppermute | solution.py:345
  310.4 8.4 %all-to-all-start.3 = ((f32[16,3,2,8,128]{4,3,2,1,0:T(8,128)}), f32[16,3,2,8,128]{4,3,2,1,0:T(8,128)S(1)}, u32[]{:S(2)}, u32[]{:S(2)}) async-start(f32[16,3,2,8,128]{4,3,2,1,0:T(8,128)} %collective-permute-done.25), calls=%async_computation.3 | async-start | bytes 786432 | tf_op jit(solution)/shard_map/all_to_all | solution.py:360
  319.7 8.2 %all-to-all-done.3 = f32[16,3,2,8,128]{4,3,2,1,0:T(8,128)S(1)} async-done(((f32[16,3,2,8,128]{4,3,2,1,0:T(8,128)}), f32[16,3,2,8,128]{4,3,2,1,0:T(8,128)S(1)}, u32[]{:S(2)}, u32[]{:S(2)}) %all-to-all-start.3) | async-done | bytes 393248 | tf_op jit(solution)/shard_map/all_to_all | solution.py:360
  (127 shorter events, 69.3 us)
Async XLA Ops:
  1.8 17.4 %collective-permute-start = (f32[2,2,128,128]{3,2,1,0:T(8,128)S(1)}, f32[2,2,128,128]{3,2,1,0:T(8,128)S(1)}, u32[]{:S(2)}, u32[]{:S(2)}) collective-permute-start(f32[2,2,128,128]{3,2,1,0:T(8,128)S(1)} %pad_maximum_fusion.2), channel_id=1, source_target_pairs={{1,0},{2,1},{3,2},{4,3},{5,4},{6,5},{7,6},{8,7},{9,8},{10,9},{11,1... | collective-permute-start | bytes 786440 | tf_op jit(solution)/shard_map/ppermute | solution.py:340
  8.1 18.3 %collective-permute-start.1 = (f32[7,128,128]{2,1,0:T(8,128)S(1)}, f32[7,128,128]{2,1,0:T(8,128)S(1)}, u32[]{:S(2)}, u32[]{:S(2)}) collective-permute-start(f32[7,128,128]{2,1,0:T(8,128)S(1)} %pad_maximum_fusion.1), channel_id=1, source_target_pairs={{0,1},{1,2},{2,3},{3,4},{4,5},{5,6},{6,7},{7,8},{8,9},{9,10},{10,1... | collective-permute-start | bytes 1376264 | tf_op jit(solution)/shard_map/ppermute | solution.py:340
  11.0 19.2 %all-to-all-start.1 = ((f32[16,2,2,8,128]{4,3,2,1,0:T(8,128)}), f32[16,2,2,8,128]{4,3,2,1,0:T(8,128)S(1)}, u32[]{:S(2)}, u32[]{:S(2)}) async-start(f32[16,2,2,8,128]{4,3,2,1,0:T(8,128)} %copy.39), calls=%async_computation.1 | async-start | bytes 524288 | tf_op jit(solution)/shard_map/all_to_all | solution.py:360
  30.2 14.9 %all-to-all-start = ((f32[16,3,2,8,128]{4,3,2,1,0:T(8,128)}), f32[16,3,2,8,128]{4,3,2,1,0:T(8,128)S(1)}, u32[]{:S(2)}, u32[]{:S(2)}) async-start(f32[16,3,2,8,128]{4,3,2,1,0:T(8,128)} %residual.1), calls=%async_computation | async-start | bytes 786432 | tf_op jit(solution)/shard_map/all_to_all | solution.py:360
  35.8 18.4 %collective-permute-start.4 = (f32[16,2,2,8,128]{4,3,2,1,0:T(8,128)S(1)}, f32[16,2,2,8,128]{4,3,2,1,0:T(8,128)}, u32[]{:S(2)}, u32[]{:S(2)}) collective-permute-start(f32[16,2,2,8,128]{4,3,2,1,0:T(8,128)S(1)} %all-to-all-done.1), channel_id=1, source_target_pairs={{0,1},{1,2},{2,3},{3,4},{4,5},{5,6},{6,7},{7,8},{8,9},{9,10},{10,1... | collective-permute-start | bytes 786440 | tf_op jit(solution)/shard_map/ppermute | solution.py:340
  39.2 19.8 %collective-permute-start.5 = (f32[16,2,2,8,128]{4,3,2,1,0:T(8,128)S(1)}, f32[16,2,2,8,128]{4,3,2,1,0:T(8,128)}, u32[]{:S(2)}, u32[]{:S(2)}) collective-permute-start(f32[16,2,2,8,128]{4,3,2,1,0:T(8,128)S(1)} %all-to-all-done.1), channel_id=1, source_target_pairs={{1,0},{2,1},{3,2},{4,3},{5,4},{6,5},{7,6},{8,7},{9,8},{10,9},{11,1... | collective-permute-start | bytes 786440 | tf_op jit(solution)/shard_map/ppermute | solution.py:340
  45.2 35.5 %collective-permute-start.8 = (f32[8,128,128]{2,1,0:T(8,128)S(1)}, f32[8,128,128]{2,1,0:T(8,128)S(1)}, u32[]{:S(2)}, u32[]{:S(2)}) collective-permute-start(f32[8,128,128]{2,1,0:T(8,128)S(1)} %pad_maximum_fusion), channel_id=1, source_target_pairs={{1,0},{2,1},{3,2},{4,3},{5,4},{6,5},{7,6},{8,7},{9,8},{10,9},{11,1... | collective-permute-start | bytes 1572872 | tf_op jit(solution)/shard_map/ppermute | solution.py:340
  48.6 32.1 %collective-permute-start.9 = (f32[8,128,128]{2,1,0:T(8,128)S(1)}, f32[8,128,128]{2,1,0:T(8,128)S(1)}, u32[]{:S(2)}, u32[]{:S(2)}) collective-permute-start(f32[8,128,128]{2,1,0:T(8,128)S(1)} %pad_maximum_fusion), channel_id=1, source_target_pairs={{0,1},{1,2},{2,3},{3,4},{4,5},{5,6},{6,7},{7,8},{8,9},{9,10},{10,1... | collective-permute-start | bytes 1572872 | tf_op jit(solution)/shard_map/ppermute | solution.py:340
  51.0 19.1 %collective-permute-start.2 = (f32[16,3,2,8,128]{4,3,2,1,0:T(8,128)S(1)}, f32[16,3,2,8,128]{4,3,2,1,0:T(8,128)S(1)}, u32[]{:S(2)}, u32[]{:S(2)}) collective-permute-start(f32[16,3,2,8,128]{4,3,2,1,0:T(8,128)S(1)} %all-to-all-done.own), channel_id=1, source_target_pairs={{0,1},{1,2},{2,3},{3,4},{4,5},{5,6},{6,7},{7,8},{8,9},{9,10},{10,1... | collective-permute-start | bytes 1179656 | tf_op jit(solution)/shard_map/ppermute | solution.py:340
  54.2 15.9 %collective-permute-start.3 = (f32[16,3,2,8,128]{4,3,2,1,0:T(8,128)S(1)}, f32[16,3,2,8,128]{4,3,2,1,0:T(8,128)S(1)}, u32[]{:S(2)}, u32[]{:S(2)}) collective-permute-start(f32[16,3,2,8,128]{4,3,2,1,0:T(8,128)S(1)} %all-to-all-done.own), channel_id=1, source_target_pairs={{1,0},{2,1},{3,2},{4,3},{5,4},{6,5},{7,6},{8,7},{9,8},{10,9},{11,1... | collective-permute-start | bytes 1179656 | tf_op jit(solution)/shard_map/ppermute | solution.py:340
  84.7 19.1 %all-to-all-start.2 = ((f32[16,3,2,8,128]{4,3,2,1,0:T(8,128)}), f32[16,3,2,8,128]{4,3,2,1,0:T(8,128)S(1)}, u32[]{:S(2)}, u32[]{:S(2)}) async-start(f32[16,3,2,8,128]{4,3,2,1,0:T(8,128)} %base.1), calls=%async_computation.2 | async-start | bytes 786432 | tf_op jit(solution)/shard_map/all_to_all | solution.py:360
  89.2 14.6 %collective-permute-start.6 = (f32[16,3,2,8,128]{4,3,2,1,0:T(8,128)S(1)}, f32[16,3,2,8,128]{4,3,2,1,0:T(8,128)S(1)}, u32[]{:S(2)}, u32[]{:S(2)}) collective-permute-start(f32[16,3,2,8,128]{4,3,2,1,0:T(8,128)S(1)} %copy-done.25), channel_id=1, source_target_pairs={{0,1},{1,2},{2,3},{3,4},{4,5},{5,6},{6,7},{7,8},{8,9},{9,10},{10,1... | collective-permute-start | bytes 1179656 | tf_op jit(solution)/shard_map/ppermute | solution.py:340
  92.6 11.2 %collective-permute-start.7 = (f32[16,3,2,8,128]{4,3,2,1,0:T(8,128)S(1)}, f32[16,3,2,8,128]{4,3,2,1,0:T(8,128)S(1)}, u32[]{:S(2)}, u32[]{:S(2)}) collective-permute-start(f32[16,3,2,8,128]{4,3,2,1,0:T(8,128)S(1)} %copy-done.25), channel_id=1, source_target_pairs={{1,0},{2,1},{3,2},{4,3},{5,4},{6,5},{7,6},{8,7},{9,8},{10,9},{11,1... | collective-permute-start | bytes 1179656 | tf_op jit(solution)/shard_map/ppermute | solution.py:340
  113.5 24.0 %collective-permute-start.11 = (f32[16,3,2,8,128]{4,3,2,1,0:T(8,128)}, f32[16,3,2,8,128]{4,3,2,1,0:T(8,128)S(1)}, u32[]{:S(2)}, u32[]{:S(2)}) collective-permute-start(f32[16,3,2,8,128]{4,3,2,1,0:T(8,128)} %get-tuple-element.16.rest_0_), channel_id=1, source_target_pairs={{0,16},{16,32},{32,48},{48,64},{64,80},{80,96},{96,112},{112,128},... | collective-permute-start | bytes 1179656 | tf_op jit(solution)/shard_map/ppermute | solution.py:345
  114.7 22.8 %collective-permute-start.10 = (f32[16,3,2,2,128]{4,3,2,1,0:T(2,128)S(1)}, f32[16,3,2,2,128]{4,3,2,1,0:T(2,128)S(1)}, u32[]{:S(2)}, u32[]{:S(2)}) collective-permute-start(f32[16,3,2,2,128]{4,3,2,1,0:T(2,128)S(1)} %get-tuple-element.27), channel_id=1, source_target_pairs={{0,17},{1,18},{2,19},{3,20},{4,21},{5,22},{6,23},{7,24},{8,25},{9,... | collective-permute-start | bytes 294920 | tf_op jit(solution)/shard_map/ppermute | solution.py:356
  118.3 19.2 %collective-permute-start.12 = (f32[16,3,2,2,128]{4,3,2,1,0:T(2,128)S(1)}, f32[16,3,2,2,128]{4,3,2,1,0:T(2,128)S(1)}, u32[]{:S(2)}, u32[]{:S(2)}) collective-permute-start(f32[16,3,2,2,128]{4,3,2,1,0:T(2,128)S(1)} %get-tuple-element.26), channel_id=1, source_target_pairs={{1,16},{2,17},{3,18},{4,19},{5,20},{6,21},{7,22},{8,23},{9,24},{10... | collective-permute-start | bytes 294920 | tf_op jit(solution)/shard_map/ppermute | solution.py:356
  142.9 36.5 %collective-permute-start.14 = (f32[16,3,2,8,128]{4,3,2,1,0:T(8,128)}, f32[16,3,2,8,128]{4,3,2,1,0:T(8,128)S(1)}, u32[]{:S(2)}, u32[]{:S(2)}) collective-permute-start(f32[16,3,2,8,128]{4,3,2,1,0:T(8,128)} %joined1.1.rest_0_), channel_id=1, source_target_pairs={{0,32},{16,48},{32,64},{48,80},{64,96},{80,112},{96,128},{112,144}... | collective-permute-start | bytes 1179656 | tf_op jit(solution)/shard_map/ppermute | solution.py:345
  144.1 35.2 %collective-permute-start.13 = (f32[16,3,2,4,128]{4,3,2,1,0:T(4,128)S(1)}, f32[16,3,2,4,128]{4,3,2,1,0:T(4,128)S(1)}, u32[]{:S(2)}, u32[]{:S(2)}) collective-permute-start(f32[16,3,2,4,128]{4,3,2,1,0:T(4,128)S(1)} %get-tuple-element.25), channel_id=1, source_target_pairs={{0,33},{1,34},{2,35},{3,36},{4,37},{5,38},{6,39},{7,40},{8,41},{9,... | collective-permute-start | bytes 589832 | tf_op jit(solution)/shard_map/ppermute | solution.py:356
  146.0 33.3 %collective-permute-start.15 = (f32[16,3,2,4,128]{4,3,2,1,0:T(4,128)S(1)}, f32[16,3,2,4,128]{4,3,2,1,0:T(4,128)S(1)}, u32[]{:S(2)}, u32[]{:S(2)}) collective-permute-start(f32[16,3,2,4,128]{4,3,2,1,0:T(4,128)S(1)} %get-tuple-element.24), channel_id=1, source_target_pairs={{1,32},{2,33},{3,34},{4,35},{5,36},{6,37},{7,38},{8,39},{9,40},{10... | collective-permute-start | bytes 589832 | tf_op jit(solution)/shard_map/ppermute | solution.py:356
  186.3 15.2 %collective-permute-start.16 = (f32[16,3,2,8,128]{4,3,2,1,0:T(8,128)}, f32[16,3,2,8,128]{4,3,2,1,0:T(8,128)S(1)}, u32[]{:S(2)}, u32[]{:S(2)}) collective-permute-start(f32[16,3,2,8,128]{4,3,2,1,0:T(8,128)} %joined2.1.own), channel_id=1, source_target_pairs={{0,1},{1,2},{2,3},{3,4},{4,5},{5,6},{6,7},{7,8},{8,9},{9,10},{10,1... | collective-permute-start | bytes 1179656 | tf_op jit(solution)/shard_map/ppermute | solution.py:340
  188.2 14.6 %collective-permute-start.17 = (f32[16,3,2,8,128]{4,3,2,1,0:T(8,128)}, f32[16,3,2,8,128]{4,3,2,1,0:T(8,128)S(1)}, u32[]{:S(2)}, u32[]{:S(2)}) collective-permute-start(f32[16,3,2,8,128]{4,3,2,1,0:T(8,128)} %joined2.1.own), channel_id=1, source_target_pairs={{1,0},{2,1},{3,2},{4,3},{5,4},{6,5},{7,6},{8,7},{9,8},{10,9},{11,1... | collective-permute-start | bytes 1179656 | tf_op jit(solution)/shard_map/ppermute | solution.py:340
  212.1 14.9 %collective-permute-start.19 = (f32[16,3,2,8,128]{4,3,2,1,0:T(8,128)}, f32[16,3,2,8,128]{4,3,2,1,0:T(8,128)S(1)}, u32[]{:S(2)}, u32[]{:S(2)}) collective-permute-start(f32[16,3,2,8,128]{4,3,2,1,0:T(8,128)} %coarse4.3.own), channel_id=1, source_target_pairs={{0,1},{1,2},{2,3},{3,4},{4,5},{5,6},{6,7},{7,8},{8,9},{9,10},{10,1... | collective-permute-start | bytes 1179656 | tf_op jit(solution)/shard_map/ppermute | solution.py:340
  214.2 14.1 %collective-permute-start.20 = (f32[16,3,2,8,128]{4,3,2,1,0:T(8,128)}, f32[16,3,2,8,128]{4,3,2,1,0:T(8,128)S(1)}, u32[]{:S(2)}, u32[]{:S(2)}) collective-permute-start(f32[16,3,2,8,128]{4,3,2,1,0:T(8,128)} %coarse4.3.own), channel_id=1, source_target_pairs={{1,0},{2,1},{3,2},{4,3},{5,4},{6,5},{7,6},{8,7},{9,8},{10,9},{11,1... | collective-permute-start | bytes 1179656 | tf_op jit(solution)/shard_map/ppermute | solution.py:340
  237.6 49.1 %copy-start.24 = (f32[16,3,2,8,128]{4,3,2,1,0:T(8,128)S(1)}, f32[16,3,2,8,128]{4,3,2,1,0:T(8,128)}, u32[]{:S(2)}) copy-start(f32[16,3,2,8,128]{4,3,2,1,0:T(8,128)} %get-tuple-element.17) | copy-start | bytes 1179652
  237.6 25.1 %collective-permute-start.22 = (f32[16,3,2,8,128]{4,3,2,1,0:T(8,128)}, f32[16,3,2,8,128]{4,3,2,1,0:T(8,128)S(1)}, u32[]{:S(2)}, u32[]{:S(2)}) collective-permute-start(f32[16,3,2,8,128]{4,3,2,1,0:T(8,128)} %coarse4.4.own), channel_id=1, source_target_pairs={{0,1},{1,2},{2,3},{3,4},{4,5},{5,6},{6,7},{7,8},{8,9},{9,10},{10,1... | collective-permute-start | bytes 1179656 | tf_op jit(solution)/shard_map/ppermute | solution.py:340
  239.7 25.4 %collective-permute-start.23 = (f32[16,3,2,8,128]{4,3,2,1,0:T(8,128)}, f32[16,3,2,8,128]{4,3,2,1,0:T(8,128)S(1)}, u32[]{:S(2)}, u32[]{:S(2)}) collective-permute-start(f32[16,3,2,8,128]{4,3,2,1,0:T(8,128)} %coarse4.4.own), channel_id=1, source_target_pairs={{1,0},{2,1},{3,2},{4,3},{5,4},{6,5},{7,6},{8,7},{9,8},{10,9},{11,1... | collective-permute-start | bytes 1179656 | tf_op jit(solution)/shard_map/ppermute | solution.py:340
  246.1 31.8 %collective-permute-start.18 = (f32[16,3,2,8,128]{4,3,2,1,0:T(8,128)S(1)}, f32[16,3,2,8,128]{4,3,2,1,0:T(8,128)S(1)}, u32[]{:S(2)}, u32[]{:S(2)}) collective-permute-start(f32[16,3,2,8,128]{4,3,2,1,0:T(8,128)S(1)} %copy-done.7), channel_id=1, source_target_pairs={{0,64},{16,80},{32,96},{48,112},{64,128},{80,144},{96,160},{112,17... | collective-permute-start | bytes 1179656 | tf_op jit(solution)/shard_map/ppermute | solution.py:345
  246.2 35.6 %collective-permute-start.21 = (f32[16,3,2,8,128]{4,3,2,1,0:T(8,128)}, f32[16,3,2,8,128]{4,3,2,1,0:T(8,128)S(1)}, u32[]{:S(2)}, u32[]{:S(2)}) collective-permute-start(f32[16,3,2,8,128]{4,3,2,1,0:T(8,128)} %coarse4.4.own), channel_id=1, source_target_pairs={{0,128},{16,144},{32,160},{48,176},{64,192},{80,208},{96,224},{112... | collective-permute-start | bytes 1179656 | tf_op jit(solution)/shard_map/ppermute | solution.py:345
  274.4 12.3 %collective-permute-start.24 = (f32[16,3,2,8,128]{4,3,2,1,0:T(8,128)}, f32[16,3,2,8,128]{4,3,2,1,0:T(8,128)S(1)}, u32[]{:S(2)}, u32[]{:S(2)}) collective-permute-start(f32[16,3,2,8,128]{4,3,2,1,0:T(8,128)} %coarse4.5), channel_id=1, source_target_pairs={{0,192},{16,208},{32,224},{48,240},{64,0},{80,16},{96,32},{112,48}... | collective-permute-start | bytes 1179656 | tf_op jit(solution)/shard_map/ppermute | solution.py:345
  287.6 22.8 %all-to-all-start.4 = ((f32[16,3,2,8,128]{4,3,2,1,0:T(8,128)}), f32[16,3,2,8,128]{4,3,2,1,0:T(8,128)S(1)}, u32[]{:S(2)}, u32[]{:S(2)}) async-start(f32[16,3,2,8,128]{4,3,2,1,0:T(8,128)} %get-tuple-element.18), calls=%async_computation.4 | async-start | bytes 786432 | tf_op jit(solution)/shard_map/all_to_all | solution.py:360
  291.4 19.0 %collective-permute-start.25 = (f32[16,3,2,8,128]{4,3,2,1,0:T(8,128)S(1)}, f32[16,3,2,8,128]{4,3,2,1,0:T(8,128)}, u32[]{:S(2)}, u32[]{:S(2)}) collective-permute-start(f32[16,3,2,8,128]{4,3,2,1,0:T(8,128)S(1)} %get-tuple-element.19), channel_id=1, source_target_pairs={{0,16},{16,32},{32,48},{48,64},{64,80},{80,96},{96,112},{112,128},... | collective-permute-start | bytes 1179656 | tf_op jit(solution)/shard_map/ppermute | solution.py:345
  310.4 17.4 %all-to-all-start.3 = ((f32[16,3,2,8,128]{4,3,2,1,0:T(8,128)}), f32[16,3,2,8,128]{4,3,2,1,0:T(8,128)S(1)}, u32[]{:S(2)}, u32[]{:S(2)}) async-start(f32[16,3,2,8,128]{4,3,2,1,0:T(8,128)} %collective-permute-done.25), calls=%async_computation.3 | async-start | bytes 786432 | tf_op jit(solution)/shard_map/all_to_all | solution.py:360
  (32 other events, 213.8 us)

commit v3 on v2

--- a/solution.py
+++ b/solution.py
@@ -7,6 +7,7 @@
 from jax.experimental.pallas import tpu as pltpu
 from jax.sharding import PartitionSpec as P
 
+
 FSTEPS = 2
 FSWEEPS = 8
 CSWEEPS = 2
@@ -17,6 +18,7 @@
 
 ROWS = 8
 UNROLL = 8
+VMEM_LIMIT = 16 << 20
 
 
 def chebyshev_weights(lower, upper, sweeps):
@@ -323,14 +325,14 @@
 SMEM = pl.BlockSpec(memory_space=pltpu.SMEM)
 
 
-def call(kernel, name, outs, scratch, flags, *operands):
+def call(kernel, outs, scratch, flags, *operands):
     return pl.pallas_call(
         kernel,
-        name=name,
         out_shape=[jax.ShapeDtypeStruct(s, jnp.float32) for s in outs],
         in_specs=[SMEM] + [VMEM] * len(operands),
         out_specs=[VMEM] * len(outs),
         scratch_shapes=[pltpu.VMEM(s, jnp.float32) for s in scratch],
+        compiler_params=pltpu.CompilerParams(vmem_limit_bytes=VMEM_LIMIT),
     )(flags, *operands)
 
 
@@ -364,7 +366,7 @@
     return open_shift(value, 1), open_shift(value, -1)
 
 
-def local(state_old, coarse_old, source, start_state, conduct, reluct, converged):
+def step(state_old, coarse_old, source, start_state, conduct, reluct, converged):
     groups = lax.axis_size("slab")
     spaces = lax.axis_size("space")
     position = (lax.axis_index("slab") - converged[0] % groups - 1) % groups
@@ -384,7 +386,7 @@
     coef24 = jnp.concatenate((coef_low, coef, coef_high), 3).transpose(1, 0, 2, 3, 4).reshape(2, nx, 3 * ROWS, 128)
     con, rel = coef24[0], coef24[1]
 
-    (res,) = call(residual_kernel, "residual", [field], [], flags, state, src, reluct, ups[0], lows[0:3], lows[6:7])
+    (res,) = call(residual_kernel, [field], [], flags, state, src, reluct, ups[0], lows[0:3], lows[6:7])
     res = turn(res)
     res_low, res_high = halo(res)
 
@@ -396,26 +398,26 @@
     slim = (nx, 3 * ROWS, 128)
     scratch = [wide, wide, slim, slim]
     total, after = call(
-        functools.partial(fine_kernel, True), "fine_first", [field, field], scratch, flags,
+        functools.partial(fine_kernel, True), [field, field], scratch, flags,
         res_low, res, res_high, con, rel,
     )
     after_low, after_high = halo(after)
     src, after = lax.optimization_barrier((src, after))
     (base,) = call(
-        base_kernel, "base", [field], [(planes + 2, 3, ny, 128)], flags,
+        base_kernel, [field], [(planes + 2, 3, ny, 128)], flags,
         state, old, src, conduct, reluct, ups[1], lows[3:6], lows[6:7], start_state, edge_high, edge_low,
     )
     base = turn(base)
 
     lead, total = call(
-        functools.partial(fine_kernel, False), "fine_second", [field, field], scratch, flags,
+        functools.partial(fine_kernel, False), [field, field], scratch, flags,
         after_low, after, after_high, con, rel, total, base,
     )
 
     def coarse(value, count):
         low, high = halo(value)
         return call(
-            functools.partial(coarse_kernel, count, None), "coarse%d" % count, [field], scratch, flags,
+            functools.partial(coarse_kernel, count, None), [field], scratch, flags,
             low, value, high, con, rel,
         )[0]
 
@@ -425,23 +427,26 @@
         low = both_shift(value[:, :, :, ROWS - rows :], steps, 1)
         high = both_shift(value[:, :, :, :rows], steps, -1)
         return call(
-            functools.partial(coarse_kernel, steps, gate), "joined%d" % steps, [field], scratch, flags,
+            functools.partial(coarse_kernel, steps, gate), [field], scratch, flags,
             low, own, high, con, rel, value,
         )[0]
 
     lead = joined(lead, 1, 3)
+    total, lead = lax.optimization_barrier((total, lead))
+    total = turn(total)
     lead = joined(lead, 2, 4)
     final, power = lead, lead
     for steps in range(4, groups, 4):
         power = coarse(power, 4)
-        final = final + jnp.where(position >= steps, ring_shift(power, steps), 0.0)
-    starts = ring_shift(final, 1)
-    ends = final - total
+        moved = ring_shift(power, steps)
+        final = final + jnp.where(position >= steps, moved, 0.0)
 
     def home(value):
-        return turn(value).transpose(1, 2, 0, 3, 4).reshape(3, planes, ny, 128)
-
-    coarse_new = home(ends) + (old - state)
+        return value.transpose(1, 2, 0, 3, 4).reshape(3, planes, ny, 128)
+
+    turned = turn(final)
+    starts = ring_shift(turned, 1)
+    coarse_new = (home(turned) - home(total)) + (old - state)
     state_new = jnp.where(position == 0, start_state, home(starts))
     return state_new[None], coarse_new[None]
 
@@ -457,7 +462,7 @@
         P(),
     )
     return jax.shard_map(
-        local,
+        step,
         mesh=mesh,
         in_specs=placed,
         out_specs=(P("slab", None, "space", None, None), P("slab", None, "space", None, None)),

time: 332 us -> 323 us (0.973)
  the two profiles are of different devices: /device:TPU:160 before, /device:TPU:6 now
where the time goes in v3:
time: 323 us; the launch traced here: 322 us
  waiting for transfers between devices  121 us (37%)
  starting transfers between devices  116 us (36%)
  Pallas kernels  44.5 us (14%)
  blocking collectives  28.3 us (9%)
  local copies, waits for them, and re-layouts  7.51 us (2%)
    ppermute x16, starting transfers between devices, open_shift(): lax.ppermute(value, 'space', [(i, i + steps) for i in range(first, last)])  63.6 us
    ppermute x16, waiting for transfers between devices, open_shift(): lax.ppermute(value, 'space', [(i, i + steps) for i in range(first, last)])  50 us
    pallas_call x9, Pallas kernels, call(): pl.pallas_call(kernel, out_shape=[jax.ShapeDtypeStruct(s, jnp.float32) fo...  44.5 us
    all_to_all x4, waiting for transfers between devices, turn(): return lax.all_to_all(value, 'space', 0, 0, tiled=True)  30.8 us
    all_to_all x4, starting transfers between devices, turn(): return lax.all_to_all(value, 'space', 0, 0, tiled=True)  29.7 us
    all_to_all x1, blocking collectives, turn(): return lax.all_to_all(value, 'space', 0, 0, tiled=True)  28.3 us
    ppermute x6, waiting for transfers between devices, ring_shift(): lax.ppermute(value, 'slab', [(i, (i + steps) % count) for i in range(coun...  25.6 us
    ppermute x4, waiting for transfers between devices, both_shift(): return lax.ppermute(value, ('slab', 'space'), pairs)  14.5 us
  transfers between devices with their start and end apart: 30, of which 18 were waited for; matrix products, arithmetic and copies ran while one was open for 1% of the time, Pallas kernels for 5%

profile of v3, /device:TPU:6, one launch (start us, length us, event | category | flops | bytes accessed | tf_op | source)
XLA Modules:
  0.0 321.9 jit_solution(16164579285932272422)
XLA Ops:
  4.1 4.7 %collective-permute-start.1 = (f32[7,128,128]{2,1,0:T(8,128)S(1)}, f32[7,128,128]{2,1,0:T(8,128)S(1)}, u32[]{:S(2)}, u32[]{:S(2)}) collective-permute-start(f32[7,128,128]{2,1,0:T(8,128)S(1)} %pad_maximum_fusion.1), channel_id=1, source_target_pairs={{0,1},{1,2},{2,3},{3,4},{4,5},{5,6},{6,7},{7,8},{8,9},{9,10},{10,1... | collective-permute-start | bytes 1376264 | tf_op jit(solution)/shard_map/ppermute | solution.py:342
  9.6 9.2 %all-to-all-start.1 = ((f32[16,2,2,8,128]{4,3,2,1,0:T(8,128)}), f32[16,2,2,8,128]{4,3,2,1,0:T(8,128)S(1)}, u32[]{:S(2)}, u32[]{:S(2)}) async-start(f32[16,2,2,8,128]{4,3,2,1,0:T(8,128)} %copy.39), calls=%async_computation.1 | async-start | bytes 524288 | tf_op jit(solution)/shard_map/all_to_all | solution.py:362
  22.2 6.6 %all-to-all-done.1 = f32[16,2,2,8,128]{4,3,2,1,0:T(8,128)S(1)} async-done(((f32[16,2,2,8,128]{4,3,2,1,0:T(8,128)}), f32[16,2,2,8,128]{4,3,2,1,0:T(8,128)S(1)}, u32[]{:S(2)}, u32[]{:S(2)}) %all-to-all-start.1) | async-done | bytes 262176 | tf_op jit(solution)/shard_map/all_to_all | solution.py:362
  28.9 6.4 %all-to-all-start = ((f32[16,3,2,8,128]{4,3,2,1,0:T(8,128)}), f32[16,3,2,8,128]{4,3,2,1,0:T(8,128)S(1)}, u32[]{:S(2)}, u32[]{:S(2)}) async-start(f32[16,3,2,8,128]{4,3,2,1,0:T(8,128)} %shard_map.86), calls=%async_computation | async-start | bytes 786432 | tf_op jit(solution)/shard_map/all_to_all | solution.py:362
  40.4 6.4 %all-to-all-done.own = f32[16,3,2,8,128]{4,3,2,1,0:T(8,128)S(1)} async-done(((f32[16,3,2,8,128]{4,3,2,1,0:T(8,128)}), f32[16,3,2,8,128]{4,3,2,1,0:T(8,128)S(1)}, u32[]{:S(2)}, u32[]{:S(2)}) %all-to-all-start) | async-done | bytes 393248 | tf_op jit(solution)/shard_map/all_to_all | solution.py:362
  48.2 4.6 %collective-permute-start.9 = (f32[8,128,128]{2,1,0:T(8,128)S(1)}, f32[8,128,128]{2,1,0:T(8,128)S(1)}, u32[]{:S(2)}, u32[]{:S(2)}) collective-permute-start(f32[8,128,128]{2,1,0:T(8,128)S(1)} %pad_maximum_fusion), channel_id=1, source_target_pairs={{0,1},{1,2},{2,3},{3,4},{4,5},{5,6},{6,7},{7,8},{8,9},{9,10},{10,1... | collective-permute-start | bytes 1572872 | tf_op jit(solution)/shard_map/ppermute | solution.py:342
  56.5 12.3 %collective-permute-done.2.low = f32[16,3,2,8,128]{4,3,2,1,0:T(8,128)S(1)} collective-permute-done((f32[16,3,2,8,128]{4,3,2,1,0:T(8,128)S(1)}, f32[16,3,2,8,128]{4,3,2,1,0:T(8,128)S(1)}, u32[]{:S(2)}, u32[]{:S(2)}) %collective-permute-start.2) | collective-permute-done | bytes 393248 | tf_op jit(solution)/shard_map/ppermute | solution.py:342
  68.8 7.1 %shard_map.87 = (f32[16,3,2,8,128]{4,3,2,1,0:T(8,128)S(1)}, f32[16,3,2,8,128]{4,3,2,1,0:T(8,128)S(1)}) custom-call(f32[5]{0:T(128)S(1)} %convert_element_type.3.flags, f32[16,3,2,8,128]{4,3,2,1,0:T(8,128)S(1)} %collective-permute-done.2.low, f32[16,3,2,8,128]{4,3,2,1,0:T(8,128)S(1)} %all-to-all-done.own, ...), custom_call_target="tpu_custom_call" | custom-call | tf_op jit(solution)/shard_map/pallas_call | solution.py:329
  79.3 8.6 %all-to-all-start.2 = ((f32[16,3,2,8,128]{4,3,2,1,0:T(8,128)}), f32[16,3,2,8,128]{4,3,2,1,0:T(8,128)S(1)}, u32[]{:S(2)}, u32[]{:S(2)}) async-start(f32[16,3,2,8,128]{4,3,2,1,0:T(8,128)} %shard_map.88), calls=%async_computation.2 | async-start | bytes 786432 | tf_op jit(solution)/shard_map/all_to_all | solution.py:362
  87.9 3.8 %collective-permute-start.6 = (f32[16,3,2,8,128]{4,3,2,1,0:T(8,128)S(1)}, f32[16,3,2,8,128]{4,3,2,1,0:T(8,128)S(1)}, u32[]{:S(2)}, u32[]{:S(2)}) collective-permute-start(f32[16,3,2,8,128]{4,3,2,1,0:T(8,128)S(1)} %copy-done.7), channel_id=1, source_target_pairs={{0,1},{1,2},{2,3},{3,4},{4,5},{5,6},{6,7},{7,8},{8,9},{9,10},{10,1... | collective-permute-start | bytes 1179656 | tf_op jit(solution)/shard_map/ppermute | solution.py:342
  93.1 6.2 %collective-permute-done.6.low = f32[16,3,2,8,128]{4,3,2,1,0:T(8,128)S(1)} collective-permute-done((f32[16,3,2,8,128]{4,3,2,1,0:T(8,128)S(1)}, f32[16,3,2,8,128]{4,3,2,1,0:T(8,128)S(1)}, u32[]{:S(2)}, u32[]{:S(2)}) %collective-permute-start.6) | collective-permute-done | bytes 393248 | tf_op jit(solution)/shard_map/ppermute | solution.py:342
  104.0 7.3 %shard_map.89 = (f32[16,3,2,8,128]{4,3,2,1,0:T(8,128)S(1)}, f32[16,3,2,8,128]{4,3,2,1,0:T(8,128)}) custom-call(f32[5]{0:T(128)S(1)} %convert_element_type.3.flags, f32[16,3,2,8,128]{4,3,2,1,0:T(8,128)S(1)} %collective-permute-done.6.low, f32[16,3,2,8,128]{4,3,2,1,0:T(8,128)S(1)} %copy-done.7, f32[16,3,2,8,128]{4,3,2,1,0:T(8,128)S(1)} %copy-done.9, ...), custom_call_target="tpu_custom_call" | custom-call | tf_op jit(solution)/shard_map/pallas_call | solution.py:329
  111.4 7.2 %collective-permute-start.10 = (f32[16,3,2,2,128]{4,3,2,1,0:T(2,128)S(1)}, f32[16,3,2,2,128]{4,3,2,1,0:T(2,128)S(1)}, u32[]{:S(2)}, u32[]{:S(2)}) collective-permute-start(f32[16,3,2,2,128]{4,3,2,1,0:T(2,128)S(1)} %get-tuple-element.29), channel_id=1, source_target_pairs={{0,17},{1,18},{2,19},{3,20},{4,21},{5,22},{6,23},{7,24},{8,25},{9,... | collective-permute-start | bytes 294920 | tf_op jit(solution)/shard_map/ppermute | solution.py:358
  120.8 4.7 %collective-permute-done.12.high = f32[16,3,2,2,128]{4,3,2,1,0:T(2,128)S(1)} collective-permute-done((f32[16,3,2,2,128]{4,3,2,1,0:T(2,128)S(1)}, f32[16,3,2,2,128]{4,3,2,1,0:T(2,128)S(1)}, u32[]{:S(2)}, u32[]{:S(2)}) %collective-permute-start.12) | collective-permute-done | bytes 98336 | tf_op jit(solution)/shard_map/ppermute | solution.py:358
  127.9 8.4 %collective-permute-start.14 = (f32[16,3,2,8,128]{4,3,2,1,0:T(8,128)S(1)}, f32[16,3,2,8,128]{4,3,2,1,0:T(8,128)S(1)}, u32[]{:S(2)}, u32[]{:S(2)}) collective-permute-start(f32[16,3,2,8,128]{4,3,2,1,0:T(8,128)S(1)} %shard_map.90.rest_0_), channel_id=1, source_target_pairs={{0,32},{16,48},{32,64},{48,80},{64,96},{80,112},{96,128},{112,144}... | collective-permute-start | bytes 1179656 | tf_op jit(solution)/shard_map/ppermute | solution.py:347
  139.8 5.4 %collective-permute-done.13.low = f32[16,3,2,4,128]{4,3,2,1,0:T(4,128)S(1)} collective-permute-done((f32[16,3,2,4,128]{4,3,2,1,0:T(4,128)S(1)}, f32[16,3,2,4,128]{4,3,2,1,0:T(4,128)S(1)}, u32[]{:S(2)}, u32[]{:S(2)}) %collective-permute-start.13) | collective-permute-done | bytes 196640 | tf_op jit(solution)/shard_map/ppermute | solution.py:358
  152.4 5.7 %collective-permute-start.16 = (f32[16,3,2,8,128]{4,3,2,1,0:T(8,128)S(1)}, f32[16,3,2,8,128]{4,3,2,1,0:T(8,128)S(1)}, u32[]{:S(2)}, u32[]{:S(2)}) collective-permute-start(f32[16,3,2,8,128]{4,3,2,1,0:T(8,128)S(1)} %shard_map.91.own), channel_id=1, source_target_pairs={{0,1},{1,2},{2,3},{3,4},{4,5},{5,6},{6,7},{7,8},{8,9},{9,10},{10,1... | collective-permute-start | bytes 1179656 | tf_op jit(solution)/shard_map/ppermute | solution.py:342
  159.4 4.0 %collective-permute-done.16.low = f32[16,3,2,8,128]{4,3,2,1,0:T(8,128)S(1)} collective-permute-done((f32[16,3,2,8,128]{4,3,2,1,0:T(8,128)S(1)}, f32[16,3,2,8,128]{4,3,2,1,0:T(8,128)S(1)}, u32[]{:S(2)}, u32[]{:S(2)}) %collective-permute-start.16) | collective-permute-done | bytes 393248 | tf_op jit(solution)/shard_map/ppermute | solution.py:342
  163.4 6.7 %collective-permute-done.17.high = f32[16,3,2,8,128]{4,3,2,1,0:T(8,128)S(1)} collective-permute-done((f32[16,3,2,8,128]{4,3,2,1,0:T(8,128)S(1)}, f32[16,3,2,8,128]{4,3,2,1,0:T(8,128)S(1)}, u32[]{:S(2)}, u32[]{:S(2)}) %collective-permute-start.17) | collective-permute-done | bytes 393248 | tf_op jit(solution)/shard_map/ppermute | solution.py:342
  170.1 6.9 %shard_map.92.own = f32[16,3,2,8,128]{4,3,2,1,0:T(8,128)S(1)} custom-call(f32[5]{0:T(128)S(1)} %convert_element_type.3.flags, f32[16,3,2,8,128]{4,3,2,1,0:T(8,128)S(1)} %collective-permute-done.16.low, f32[16,3,2,8,128]{4,3,2,1,0:T(8,128)S(1)} %shard_map.91.own, f32[16,3,2,8,128]{4,3,2,1,0:T(8,128)S(1)} %collective-permute-done.17.high, ...), custom_call_target="tpu_custom_call" | custom-call | tf_op jit(solution)/shard_map/pallas_call | solution.py:329
  177.0 23.9 %collective-permute-start.19 = (f32[16,3,2,8,128]{4,3,2,1,0:T(8,128)S(1)}, f32[16,3,2,8,128]{4,3,2,1,0:T(8,128)S(1)}, u32[]{:S(2)}, u32[]{:S(2)}) collective-permute-start(f32[16,3,2,8,128]{4,3,2,1,0:T(8,128)S(1)} %shard_map.92.own), channel_id=1, source_target_pairs={{0,1},{1,2},{2,3},{3,4},{4,5},{5,6},{6,7},{7,8},{8,9},{9,10},{10,1... | collective-permute-start | bytes 1179656 | tf_op jit(solution)/shard_map/ppermute | solution.py:342
  202.4 6.2 %collective-permute-done.19.low = f32[16,3,2,8,128]{4,3,2,1,0:T(8,128)S(1)} collective-permute-done((f32[16,3,2,8,128]{4,3,2,1,0:T(8,128)S(1)}, f32[16,3,2,8,128]{4,3,2,1,0:T(8,128)S(1)}, u32[]{:S(2)}, u32[]{:S(2)}) %collective-permute-start.19) | collective-permute-done | bytes 393248 | tf_op jit(solution)/shard_map/ppermute | solution.py:342
  208.5 4.1 %collective-permute-done.20.high = f32[16,3,2,8,128]{4,3,2,1,0:T(8,128)S(1)} collective-permute-done((f32[16,3,2,8,128]{4,3,2,1,0:T(8,128)S(1)}, f32[16,3,2,8,128]{4,3,2,1,0:T(8,128)S(1)}, u32[]{:S(2)}, u32[]{:S(2)}) %collective-permute-start.20) | collective-permute-done | bytes 393248 | tf_op jit(solution)/shard_map/ppermute | solution.py:342
  212.7 6.9 %shard_map.93.own = f32[16,3,2,8,128]{4,3,2,1,0:T(8,128)S(1)} custom-call(f32[5]{0:T(128)S(1)} %convert_element_type.3.flags, f32[16,3,2,8,128]{4,3,2,1,0:T(8,128)S(1)} %collective-permute-done.19.low, f32[16,3,2,8,128]{4,3,2,1,0:T(8,128)S(1)} %shard_map.92.own, f32[16,3,2,8,128]{4,3,2,1,0:T(8,128)S(1)} %collective-permute-done.20.high, ...), custom_call_target="tpu_custom_call" | custom-call | tf_op jit(solution)/shard_map/pallas_call | solution.py:329
  219.6 4.3 %collective-permute-start.22 = (f32[16,3,2,8,128]{4,3,2,1,0:T(8,128)S(1)}, f32[16,3,2,8,128]{4,3,2,1,0:T(8,128)S(1)}, u32[]{:S(2)}, u32[]{:S(2)}) collective-permute-start(f32[16,3,2,8,128]{4,3,2,1,0:T(8,128)S(1)} %shard_map.93.own), channel_id=1, source_target_pairs={{0,1},{1,2},{2,3},{3,4},{4,5},{5,6},{6,7},{7,8},{8,9},{9,10},{10,1... | collective-permute-start | bytes 1179656 | tf_op jit(solution)/shard_map/ppermute | solution.py:342
  230.7 4.1 %collective-permute-done.23.high = f32[16,3,2,8,128]{4,3,2,1,0:T(8,128)S(1)} collective-permute-done((f32[16,3,2,8,128]{4,3,2,1,0:T(8,128)S(1)}, f32[16,3,2,8,128]{4,3,2,1,0:T(8,128)S(1)}, u32[]{:S(2)}, u32[]{:S(2)}) %collective-permute-start.23) | collective-permute-done | bytes 393248 | tf_op jit(solution)/shard_map/ppermute | solution.py:342
  234.8 6.9 %shard_map.94 = f32[16,3,2,8,128]{4,3,2,1,0:T(8,128)S(1)} custom-call(f32[5]{0:T(128)S(1)} %convert_element_type.3.flags, f32[16,3,2,8,128]{4,3,2,1,0:T(8,128)S(1)} %collective-permute-done.22.low, f32[16,3,2,8,128]{4,3,2,1,0:T(8,128)S(1)} %shard_map.93.own, f32[16,3,2,8,128]{4,3,2,1,0:T(8,128)S(1)} %collective-permute-done.23.high, ...), custom_call_target="tpu_custom_call" | custom-call | tf_op jit(solution)/shard_map/pallas_call | solution.py:329
  241.8 10.5 %collective-permute-done.21 = f32[16,3,2,8,128]{4,3,2,1,0:T(8,128)} collective-permute-done((f32[16,3,2,8,128]{4,3,2,1,0:T(8,128)S(1)}, f32[16,3,2,8,128]{4,3,2,1,0:T(8,128)}, u32[]{:S(2)}, u32[]{:S(2)}) %collective-permute-start.21) | collective-permute-done | bytes 393248 | tf_op jit(solution)/shard_map/ppermute | solution.py:347
  252.3 15.1 %collective-permute-done.24 = f32[16,3,2,8,128]{4,3,2,1,0:T(8,128)S(1)} collective-permute-done((f32[16,3,2,8,128]{4,3,2,1,0:T(8,128)S(1)}, f32[16,3,2,8,128]{4,3,2,1,0:T(8,128)S(1)}, u32[]{:S(2)}, u32[]{:S(2)}) %collective-permute-start.24) | collective-permute-done | bytes 393248 | tf_op jit(solution)/shard_map/ppermute | solution.py:347
  268.5 28.3 %all_to_all.25 = f32[16,3,2,8,128]{4,3,2,1,0:T(8,128)S(1)} all-to-all(f32[16,3,2,8,128]{4,3,2,1,0:T(8,128)S(1)} %select_add_fusion), channel_id=1, replica_groups=mesh['slab'=16,'space'=16] {'space'}, dimensions={0} | all-to-all | bytes 786432 | tf_op jit(solution)/shard_map/all_to_all | solution.py:362
  296.8 5.6 %all-to-all-start.4 = ((f32[16,3,2,8,128]{4,3,2,1,0:T(8,128)}), f32[16,3,2,8,128]{4,3,2,1,0:T(8,128)S(1)}, u32[]{:S(2)}, u32[]{:S(2)}) async-start(f32[16,3,2,8,128]{4,3,2,1,0:T(8,128)} %get-tuple-element.21), calls=%async_computation.4 | async-start | bytes 786432 | tf_op jit(solution)/shard_map/all_to_all | solution.py:362
  302.5 17.8 %all-to-all-done.4 = f32[16,3,2,8,128]{4,3,2,1,0:T(8,128)S(1)} async-done(((f32[16,3,2,8,128]{4,3,2,1,0:T(8,128)}), f32[16,3,2,8,128]{4,3,2,1,0:T(8,128)S(1)}, u32[]{:S(2)}, u32[]{:S(2)}) %all-to-all-start.4) | async-done | bytes 393248 | tf_op jit(solution)/shard_map/all_to_all | solution.py:362
  (86 shorter events, 54.3 us)
Async XLA Ops:
  1.8 17.7 %collective-permute-start = (f32[2,2,128,128]{3,2,1,0:T(8,128)S(1)}, f32[2,2,128,128]{3,2,1,0:T(8,128)S(1)}, u32[]{:S(2)}, u32[]{:S(2)}) collective-permute-start(f32[2,2,128,128]{3,2,1,0:T(8,128)S(1)} %pad_maximum_fusion.2), channel_id=1, source_target_pairs={{1,0},{2,1},{3,2},{4,3},{5,4},{6,5},{7,6},{8,7},{9,8},{10,9},{11,1... | collective-permute-start | bytes 786440 | tf_op jit(solution)/shard_map/ppermute | solution.py:342
  4.1 15.5 %collective-permute-start.1 = (f32[7,128,128]{2,1,0:T(8,128)S(1)}, f32[7,128,128]{2,1,0:T(8,128)S(1)}, u32[]{:S(2)}, u32[]{:S(2)}) collective-permute-start(f32[7,128,128]{2,1,0:T(8,128)S(1)} %pad_maximum_fusion.1), channel_id=1, source_target_pairs={{0,1},{1,2},{2,3},{3,4},{4,5},{5,6},{6,7},{7,8},{8,9},{9,10},{10,1... | collective-permute-start | bytes 1376264 | tf_op jit(solution)/shard_map/ppermute | solution.py:342
  9.6 19.3 %all-to-all-start.1 = ((f32[16,2,2,8,128]{4,3,2,1,0:T(8,128)}), f32[16,2,2,8,128]{4,3,2,1,0:T(8,128)S(1)}, u32[]{:S(2)}, u32[]{:S(2)}) async-start(f32[16,2,2,8,128]{4,3,2,1,0:T(8,128)} %copy.39), calls=%async_computation.1 | async-start | bytes 524288 | tf_op jit(solution)/shard_map/all_to_all | solution.py:362
  22.2 24.6 %copy-start.1 = (f32[3,2,128,128]{3,2,1,0:T(8,128)S(1)}, f32[3,2,128,128]{3,2,1,0:T(8,128)}, u32[]{:S(2)}) copy-start(f32[3,2,128,128]{3,2,1,0:T(8,128)} %begin) | copy-start | bytes 1179652
  28.9 18.0 %all-to-all-start = ((f32[16,3,2,8,128]{4,3,2,1,0:T(8,128)}), f32[16,3,2,8,128]{4,3,2,1,0:T(8,128)S(1)}, u32[]{:S(2)}, u32[]{:S(2)}) async-start(f32[16,3,2,8,128]{4,3,2,1,0:T(8,128)} %shard_map.86), calls=%async_computation | async-start | bytes 786432 | tf_op jit(solution)/shard_map/all_to_all | solution.py:362
  35.2 19.8 %collective-permute-start.4 = (f32[16,2,2,8,128]{4,3,2,1,0:T(8,128)S(1)}, f32[16,2,2,8,128]{4,3,2,1,0:T(8,128)S(1)}, u32[]{:S(2)}, u32[]{:S(2)}) collective-permute-start(f32[16,2,2,8,128]{4,3,2,1,0:T(8,128)S(1)} %all-to-all-done.1), channel_id=1, source_target_pairs={{0,1},{1,2},{2,3},{3,4},{4,5},{5,6},{6,7},{7,8},{8,9},{9,10},{10,1... | collective-permute-start | bytes 786440 | tf_op jit(solution)/shard_map/ppermute | solution.py:342
  39.1 17.3 %collective-permute-start.5 = (f32[16,2,2,8,128]{4,3,2,1,0:T(8,128)S(1)}, f32[16,2,2,8,128]{4,3,2,1,0:T(8,128)S(1)}, u32[]{:S(2)}, u32[]{:S(2)}) collective-permute-start(f32[16,2,2,8,128]{4,3,2,1,0:T(8,128)S(1)} %all-to-all-done.1), channel_id=1, source_target_pairs={{1,0},{2,1},{3,2},{4,3},{5,4},{6,5},{7,6},{8,7},{9,8},{10,9},{11,1... | collective-permute-start | bytes 786440 | tf_op jit(solution)/shard_map/ppermute | solution.py:342
  46.9 29.8 %collective-permute-start.8 = (f32[8,128,128]{2,1,0:T(8,128)S(1)}, f32[8,128,128]{2,1,0:T(8,128)S(1)}, u32[]{:S(2)}, u32[]{:S(2)}) collective-permute-start(f32[8,128,128]{2,1,0:T(8,128)S(1)} %pad_maximum_fusion), channel_id=1, source_target_pairs={{1,0},{2,1},{3,2},{4,3},{5,4},{6,5},{7,6},{8,7},{9,8},{10,9},{11,1... | collective-permute-start | bytes 1572872 | tf_op jit(solution)/shard_map/ppermute | solution.py:342
  48.2 28.5 %collective-permute-start.9 = (f32[8,128,128]{2,1,0:T(8,128)S(1)}, f32[8,128,128]{2,1,0:T(8,128)S(1)}, u32[]{:S(2)}, u32[]{:S(2)}) collective-permute-start(f32[8,128,128]{2,1,0:T(8,128)S(1)} %pad_maximum_fusion), channel_id=1, source_target_pairs={{0,1},{1,2},{2,3},{3,4},{4,5},{5,6},{6,7},{7,8},{8,9},{9,10},{10,1... | collective-permute-start | bytes 1572872 | tf_op jit(solution)/shard_map/ppermute | solution.py:342
  52.8 16.0 %collective-permute-start.2 = (f32[16,3,2,8,128]{4,3,2,1,0:T(8,128)S(1)}, f32[16,3,2,8,128]{4,3,2,1,0:T(8,128)S(1)}, u32[]{:S(2)}, u32[]{:S(2)}) collective-permute-start(f32[16,3,2,8,128]{4,3,2,1,0:T(8,128)S(1)} %all-to-all-done.own), channel_id=1, source_target_pairs={{0,1},{1,2},{2,3},{3,4},{4,5},{5,6},{6,7},{7,8},{8,9},{9,10},{10,1... | collective-permute-start | bytes 1179656 | tf_op jit(solution)/shard_map/ppermute | solution.py:342
  55.1 13.7 %collective-permute-start.3 = (f32[16,3,2,8,128]{4,3,2,1,0:T(8,128)S(1)}, f32[16,3,2,8,128]{4,3,2,1,0:T(8,128)S(1)}, u32[]{:S(2)}, u32[]{:S(2)}) collective-permute-start(f32[16,3,2,8,128]{4,3,2,1,0:T(8,128)S(1)} %all-to-all-done.own), channel_id=1, source_target_pairs={{1,0},{2,1},{3,2},{4,3},{5,4},{6,5},{7,6},{8,7},{9,8},{10,9},{11,1... | collective-permute-start | bytes 1179656 | tf_op jit(solution)/shard_map/ppermute | solution.py:342
  79.3 8.6 %copy-start.7 = (f32[16,3,2,8,128]{4,3,2,1,0:T(8,128)S(1)}, f32[16,3,2,8,128]{4,3,2,1,0:T(8,128)}, u32[]{:S(2)}) copy-start(f32[16,3,2,8,128]{4,3,2,1,0:T(8,128)} %copy-done.6) | copy-start | bytes 1179652
  79.3 23.7 %all-to-all-start.2 = ((f32[16,3,2,8,128]{4,3,2,1,0:T(8,128)}), f32[16,3,2,8,128]{4,3,2,1,0:T(8,128)S(1)}, u32[]{:S(2)}, u32[]{:S(2)}) async-start(f32[16,3,2,8,128]{4,3,2,1,0:T(8,128)} %shard_map.88), calls=%async_computation.2 | async-start | bytes 786432 | tf_op jit(solution)/shard_map/all_to_all | solution.py:362
  87.9 11.4 %collective-permute-start.6 = (f32[16,3,2,8,128]{4,3,2,1,0:T(8,128)S(1)}, f32[16,3,2,8,128]{4,3,2,1,0:T(8,128)S(1)}, u32[]{:S(2)}, u32[]{:S(2)}) collective-permute-start(f32[16,3,2,8,128]{4,3,2,1,0:T(8,128)S(1)} %copy-done.7), channel_id=1, source_target_pairs={{0,1},{1,2},{2,3},{3,4},{4,5},{5,6},{6,7},{7,8},{8,9},{9,10},{10,1... | collective-permute-start | bytes 1179656 | tf_op jit(solution)/shard_map/ppermute | solution.py:342
  91.8 10.5 %collective-permute-start.7 = (f32[16,3,2,8,128]{4,3,2,1,0:T(8,128)S(1)}, f32[16,3,2,8,128]{4,3,2,1,0:T(8,128)S(1)}, u32[]{:S(2)}, u32[]{:S(2)}) collective-permute-start(f32[16,3,2,8,128]{4,3,2,1,0:T(8,128)S(1)} %copy-done.7), channel_id=1, source_target_pairs={{1,0},{2,1},{3,2},{4,3},{5,4},{6,5},{7,6},{8,7},{9,8},{10,9},{11,1... | collective-permute-start | bytes 1179656 | tf_op jit(solution)/shard_map/ppermute | solution.py:342
  111.3 14.2 %collective-permute-start.11 = (f32[16,3,2,8,128]{4,3,2,1,0:T(8,128)S(1)}, f32[16,3,2,8,128]{4,3,2,1,0:T(8,128)S(1)}, u32[]{:S(2)}, u32[]{:S(2)}) collective-permute-start(f32[16,3,2,8,128]{4,3,2,1,0:T(8,128)S(1)} %get-tuple-element.19.rest_0_), channel_id=1, source_target_pairs={{0,16},{16,32},{32,48},{48,64},{64,80},{80,96},{96,112},{112,128},... | collective-permute-start | bytes 1179656 | tf_op jit(solution)/shard_map/ppermute | solution.py:347
  111.4 9.4 %collective-permute-start.10 = (f32[16,3,2,2,128]{4,3,2,1,0:T(2,128)S(1)}, f32[16,3,2,2,128]{4,3,2,1,0:T(2,128)S(1)}, u32[]{:S(2)}, u32[]{:S(2)}) collective-permute-start(f32[16,3,2,2,128]{4,3,2,1,0:T(2,128)S(1)} %get-tuple-element.29), channel_id=1, source_target_pairs={{0,17},{1,18},{2,19},{3,20},{4,21},{5,22},{6,23},{7,24},{8,25},{9,... | collective-permute-start | bytes 294920 | tf_op jit(solution)/shard_map/ppermute | solution.py:358
  118.6 6.9 %collective-permute-start.12 = (f32[16,3,2,2,128]{4,3,2,1,0:T(2,128)S(1)}, f32[16,3,2,2,128]{4,3,2,1,0:T(2,128)S(1)}, u32[]{:S(2)}, u32[]{:S(2)}) collective-permute-start(f32[16,3,2,2,128]{4,3,2,1,0:T(2,128)S(1)} %get-tuple-element.28), channel_id=1, source_target_pairs={{1,16},{2,17},{3,18},{4,19},{5,20},{6,21},{7,22},{8,23},{9,24},{10... | collective-permute-start | bytes 294920 | tf_op jit(solution)/shard_map/ppermute | solution.py:358
  127.9 20.8 %collective-permute-start.14 = (f32[16,3,2,8,128]{4,3,2,1,0:T(8,128)S(1)}, f32[16,3,2,8,128]{4,3,2,1,0:T(8,128)S(1)}, u32[]{:S(2)}, u32[]{:S(2)}) collective-permute-start(f32[16,3,2,8,128]{4,3,2,1,0:T(8,128)S(1)} %shard_map.90.rest_0_), channel_id=1, source_target_pairs={{0,32},{16,48},{32,64},{48,80},{64,96},{80,112},{96,128},{112,144}... | collective-permute-start | bytes 1179656 | tf_op jit(solution)/shard_map/ppermute | solution.py:347
  136.3 8.9 %collective-permute-start.13 = (f32[16,3,2,4,128]{4,3,2,1,0:T(4,128)S(1)}, f32[16,3,2,4,128]{4,3,2,1,0:T(4,128)S(1)}, u32[]{:S(2)}, u32[]{:S(2)}) collective-permute-start(f32[16,3,2,4,128]{4,3,2,1,0:T(4,128)S(1)} %get-tuple-element.27), channel_id=1, source_target_pairs={{0,33},{1,34},{2,35},{3,36},{4,37},{5,38},{6,39},{7,40},{8,41},{9,... | collective-permute-start | bytes 589832 | tf_op jit(solution)/shard_map/ppermute | solution.py:358
  138.5 10.2 %collective-permute-start.15 = (f32[16,3,2,4,128]{4,3,2,1,0:T(4,128)S(1)}, f32[16,3,2,4,128]{4,3,2,1,0:T(4,128)S(1)}, u32[]{:S(2)}, u32[]{:S(2)}) collective-permute-start(f32[16,3,2,4,128]{4,3,2,1,0:T(4,128)S(1)} %get-tuple-element.26), channel_id=1, source_target_pairs={{1,32},{2,33},{3,34},{4,35},{5,36},{6,37},{7,38},{8,39},{9,40},{10... | collective-permute-start | bytes 589832 | tf_op jit(solution)/shard_map/ppermute | solution.py:358
  152.4 10.9 %collective-permute-start.16 = (f32[16,3,2,8,128]{4,3,2,1,0:T(8,128)S(1)}, f32[16,3,2,8,128]{4,3,2,1,0:T(8,128)S(1)}, u32[]{:S(2)}, u32[]{:S(2)}) collective-permute-start(f32[16,3,2,8,128]{4,3,2,1,0:T(8,128)S(1)} %shard_map.91.own), channel_id=1, source_target_pairs={{0,1},{1,2},{2,3},{3,4},{4,5},{5,6},{6,7},{7,8},{8,9},{9,10},{10,1... | collective-permute-start | bytes 1179656 | tf_op jit(solution)/shard_map/ppermute | solution.py:342
  158.1 12.0 %collective-permute-start.17 = (f32[16,3,2,8,128]{4,3,2,1,0:T(8,128)S(1)}, f32[16,3,2,8,128]{4,3,2,1,0:T(8,128)S(1)}, u32[]{:S(2)}, u32[]{:S(2)}) collective-permute-start(f32[16,3,2,8,128]{4,3,2,1,0:T(8,128)S(1)} %shard_map.91.own), channel_id=1, source_target_pairs={{1,0},{2,1},{3,2},{4,3},{5,4},{6,5},{7,6},{8,7},{9,8},{10,9},{11,1... | collective-permute-start | bytes 1179656 | tf_op jit(solution)/shard_map/ppermute | solution.py:342
  177.0 31.5 %collective-permute-start.19 = (f32[16,3,2,8,128]{4,3,2,1,0:T(8,128)S(1)}, f32[16,3,2,8,128]{4,3,2,1,0:T(8,128)S(1)}, u32[]{:S(2)}, u32[]{:S(2)}) collective-permute-start(f32[16,3,2,8,128]{4,3,2,1,0:T(8,128)S(1)} %shard_map.92.own), channel_id=1, source_target_pairs={{0,1},{1,2},{2,3},{3,4},{4,5},{5,6},{6,7},{7,8},{8,9},{9,10},{10,1... | collective-permute-start | bytes 1179656 | tf_op jit(solution)/shard_map/ppermute | solution.py:342
  200.9 11.8 %collective-permute-start.20 = (f32[16,3,2,8,128]{4,3,2,1,0:T(8,128)S(1)}, f32[16,3,2,8,128]{4,3,2,1,0:T(8,128)S(1)}, u32[]{:S(2)}, u32[]{:S(2)}) collective-permute-start(f32[16,3,2,8,128]{4,3,2,1,0:T(8,128)S(1)} %shard_map.92.own), channel_id=1, source_target_pairs={{1,0},{2,1},{3,2},{4,3},{5,4},{6,5},{7,6},{8,7},{9,8},{10,9},{11,1... | collective-permute-start | bytes 1179656 | tf_op jit(solution)/shard_map/ppermute | solution.py:342
  219.6 11.1 %collective-permute-start.22 = (f32[16,3,2,8,128]{4,3,2,1,0:T(8,128)S(1)}, f32[16,3,2,8,128]{4,3,2,1,0:T(8,128)S(1)}, u32[]{:S(2)}, u32[]{:S(2)}) collective-permute-start(f32[16,3,2,8,128]{4,3,2,1,0:T(8,128)S(1)} %shard_map.93.own), channel_id=1, source_target_pairs={{0,1},{1,2},{2,3},{3,4},{4,5},{5,6},{6,7},{7,8},{8,9},{9,10},{10,1... | collective-permute-start | bytes 1179656 | tf_op jit(solution)/shard_map/ppermute | solution.py:342
  223.9 10.9 %collective-permute-start.23 = (f32[16,3,2,8,128]{4,3,2,1,0:T(8,128)S(1)}, f32[16,3,2,8,128]{4,3,2,1,0:T(8,128)S(1)}, u32[]{:S(2)}, u32[]{:S(2)}) collective-permute-start(f32[16,3,2,8,128]{4,3,2,1,0:T(8,128)S(1)} %shard_map.93.own), channel_id=1, source_target_pairs={{1,0},{2,1},{3,2},{4,3},{5,4},{6,5},{7,6},{8,7},{9,8},{10,9},{11,1... | collective-permute-start | bytes 1179656 | tf_op jit(solution)/shard_map/ppermute | solution.py:342
  225.2 16.6 %collective-permute-start.18 = (f32[16,3,2,8,128]{4,3,2,1,0:T(8,128)S(1)}, f32[16,3,2,8,128]{4,3,2,1,0:T(8,128)}, u32[]{:S(2)}, u32[]{:S(2)}) collective-permute-start(f32[16,3,2,8,128]{4,3,2,1,0:T(8,128)S(1)} %shard_map.92.own), channel_id=1, source_target_pairs={{0,64},{16,80},{32,96},{48,112},{64,128},{80,144},{96,160},{112,17... | collective-permute-start | bytes 1179656 | tf_op jit(solution)/shard_map/ppermute | solution.py:347
  225.3 27.1 %collective-permute-start.21 = (f32[16,3,2,8,128]{4,3,2,1,0:T(8,128)S(1)}, f32[16,3,2,8,128]{4,3,2,1,0:T(8,128)}, u32[]{:S(2)}, u32[]{:S(2)}) collective-permute-start(f32[16,3,2,8,128]{4,3,2,1,0:T(8,128)S(1)} %shard_map.93.own), channel_id=1, source_target_pairs={{0,128},{16,144},{32,160},{48,176},{64,192},{80,208},{96,224},{112... | collective-permute-start | bytes 1179656 | tf_op jit(solution)/shard_map/ppermute | solution.py:347
  241.7 25.7 %collective-permute-start.24 = (f32[16,3,2,8,128]{4,3,2,1,0:T(8,128)S(1)}, f32[16,3,2,8,128]{4,3,2,1,0:T(8,128)S(1)}, u32[]{:S(2)}, u32[]{:S(2)}) collective-permute-start(f32[16,3,2,8,128]{4,3,2,1,0:T(8,128)S(1)} %shard_map.94), channel_id=1, source_target_pairs={{0,192},{16,208},{32,224},{48,240},{64,0},{80,16},{96,32},{112,48}... | collective-permute-start | bytes 1179656 | tf_op jit(solution)/shard_map/ppermute | solution.py:347
  296.8 23.5 %all-to-all-start.4 = ((f32[16,3,2,8,128]{4,3,2,1,0:T(8,128)}), f32[16,3,2,8,128]{4,3,2,1,0:T(8,128)S(1)}, u32[]{:S(2)}, u32[]{:S(2)}) async-start(f32[16,3,2,8,128]{4,3,2,1,0:T(8,128)} %get-tuple-element.21), calls=%async_computation.4 | async-start | bytes 786432 | tf_op jit(solution)/shard_map/all_to_all | solution.py:362
  302.4 18.7 %collective-permute-start.25 = (f32[16,3,2,8,128]{4,3,2,1,0:T(8,128)S(1)}, f32[16,3,2,8,128]{4,3,2,1,0:T(8,128)S(1)}, u32[]{:S(2)}, u32[]{:S(2)}) collective-permute-start(f32[16,3,2,8,128]{4,3,2,1,0:T(8,128)S(1)} %all_to_all.25), channel_id=1, source_target_pairs={{0,16},{16,32},{32,48},{48,64},{64,80},{80,96},{96,112},{112,128},... | collective-permute-start | bytes 1179656 | tf_op jit(solution)/shard_map/ppermute | solution.py:347
  (11 other events, 25.2 us)
